TPU v7x, 256 devices: a whole 4x4x8 slice. The times are simulated.
256 devices in a mesh: grp: 8 (over x_hi, y), blk: 32 (over x_lo, z, core).
Axes of the slice: x: 4 (x_hi: 2, x_lo: 2; x = x_hi * 2 + x_lo), y: 4, z: 8, core: 2. Of those that a mesh axis runs over, the one named last changes fastest.
Arguments:
- tokens: bfloat16 [32768, 2048], P(('grp', 'blk')), may hold values from -6 to 6
- d_out: bfloat16 [32768, 2048], P(('grp', 'blk')), may hold values from -24 to 24
- expert_ids: int32 [32768, 6], P(('grp', 'blk')), may hold values from 0 to 31, all different within a row; in each aligned block of 128 rows (0 to 127, 128 to 255, ...) at most 26 rows name the same one
- gate_values: bfloat16 [32768, 6], P(('grp', 'blk')), may hold values from 0.049804688 to 0.44921875
- saved_gate_pre: bfloat16 [32768, 6, 704], P(('grp', 'blk')), may hold values from -6 to 6
- saved_up_pre: bfloat16 [32768, 6, 704], P(('grp', 'blk')), may hold values from -6 to 6
- w_gate: bfloat16 [32, 2048, 704], P('blk'), may hold values from -0.125 to 0.125
- w_up: bfloat16 [32, 2048, 704], P('blk'), may hold values from -0.125 to 0.125
- w_down: bfloat16 [32, 704, 2048], P('blk'), may hold values from -0.21875 to 0.21875
Outputs:
- d_tokens: bfloat16 [32768, 2048], P(('grp', 'blk'))
- d_w_gate: bfloat16 [32, 2048, 704], P('blk', 'grp')
- d_w_up: bfloat16 [32, 2048, 704], P('blk', 'grp')
- d_w_down: bfloat16 [32, 704, 2048], P('blk', None, 'grp')
Inputs may be any that keep to these rules, and one draw needn't show every extreme that they name: `expert_ids`: within the 128 rows of one device no expert is named more than 26 times, a bound that some block reaches; the 6 ids of a token differ.
All inputs are finite; a program needn't handle non-finite values.
Results may differ from a plain program's by a relative error of at most 0.0057.
Values may be sent and summed in bfloat16 or wider, within the bound.
A program may use at most 192 MiB of HBM per device.

v0:
```python
import jax
import jax.numpy as jnp
from jax import lax
from jax.sharding import PartitionSpec as P


def expert_side(cotangents, weights, gate_pre, up_pre, w_gate, w_up, w_down):
    sigmoid_gate = jax.nn.sigmoid(gate_pre)
    active = gate_pre * sigmoid_gate
    scale_col = weights[:, :, None]
    scaled_hidden = (scale_col * active * up_pre).astype(jnp.bfloat16)
    back_hidden = scale_col * jnp.einsum(
        "erd,efd->erf", cotangents, w_down, preferred_element_type=jnp.float32
    )
    grad_gate = (
        back_hidden * up_pre * sigmoid_gate * (1.0 + gate_pre * (1.0 - sigmoid_gate))
    ).astype(jnp.bfloat16)
    grad_up = (back_hidden * active).astype(jnp.bfloat16)
    route_grad = (
        jnp.einsum("erf,edf->erd", grad_gate, w_gate, preferred_element_type=jnp.float32)
        + jnp.einsum("erf,edf->erd", grad_up, w_up, preferred_element_type=jnp.float32)
    ).astype(jnp.bfloat16)
    return (route_grad, grad_gate, grad_up, scaled_hidden)


def per_device(
    tokens, d_out, expert_ids, gate_values, saved_gate_pre, saved_up_pre, w_gate, w_up, w_down
):
    tok_dev, model_width = tokens.shape
    top_count = expert_ids.shape[1]
    ffw_width = saved_gate_pre.shape[2]
    blk_count = lax.axis_size("blk")
    exp_dev = w_gate.shape[0]
    expert_count = exp_dev * blk_count
    slot_count = 13 * tok_dev // (2 * expert_count)
    buffer_rows = expert_count * slot_count
    route_count = tok_dev * top_count
    flat_ids = expert_ids.reshape(-1)
    onehot = (flat_ids[:, None] == jnp.arange(expert_count, dtype=jnp.int32)[None, :]).astype(
        jnp.int32
    )
    before = jnp.cumsum(onehot, axis=0) - onehot
    slot_index = jnp.sum(before * onehot, axis=1)
    target = flat_ids * slot_count + slot_index
    slot_route = (
        jnp.zeros((buffer_rows,), jnp.int32)
        .at[target]
        .set(jnp.arange(route_count, dtype=jnp.int32))
    )
    filled = jnp.zeros((buffer_rows,), jnp.bool_).at[target].set(True)
    token_row = slot_route // top_count

    def pick(table, rows):
        taken = table[rows]
        return jnp.where(
            filled.reshape((buffer_rows,) + (1,) * (taken.ndim - 1)), taken, jnp.zeros_like(taken)
        )

    send_inputs = pick(tokens, token_row)
    send_grads = pick(d_out, token_row)
    send_gate_pre = pick(saved_gate_pre.reshape(route_count, ffw_width), slot_route)
    send_up_pre = pick(saved_up_pre.reshape(route_count, ffw_width), slot_route)
    send_gate = pick(gate_values.reshape(-1), slot_route)
    per_peer = exp_dev * slot_count
    recv_inputs, recv_grads, recv_gpre, recv_upre, recv_gate = (
        lax.all_to_all(
            send_inputs.reshape(blk_count, per_peer, model_width),
            "blk",
            split_axis=0,
            concat_axis=0,
            tiled=True,
        ),
        lax.all_to_all(
            send_grads.reshape(blk_count, per_peer, model_width),
            "blk",
            split_axis=0,
            concat_axis=0,
            tiled=True,
        ),
        lax.all_to_all(
            send_gate_pre.reshape(blk_count, per_peer, ffw_width),
            "blk",
            split_axis=0,
            concat_axis=0,
            tiled=True,
        ),
        lax.all_to_all(
            send_up_pre.reshape(blk_count, per_peer, ffw_width),
            "blk",
            split_axis=0,
            concat_axis=0,
            tiled=True,
        ),
        lax.all_to_all(
            send_gate.reshape(blk_count, per_peer), "blk", split_axis=0, concat_axis=0, tiled=True
        ),
    )
    local_rows = blk_count * slot_count

    def to_expert(array):
        shaped = array.reshape((blk_count, exp_dev, slot_count) + array.shape[2:])
        moved = jnp.swapaxes(shaped, 0, 1)
        return moved.reshape((exp_dev, local_rows) + array.shape[2:])

    inputs = to_expert(recv_inputs)
    cotangents = to_expert(recv_grads)
    gate_pre = to_expert(recv_gpre).astype(jnp.float32)
    up_pre = to_expert(recv_upre).astype(jnp.float32)
    weights = to_expert(recv_gate).astype(jnp.float32)
    route_grad, grad_gate, grad_up, scaled_hidden = expert_side(
        cotangents, weights, gate_pre, up_pre, w_gate, w_up, w_down
    )
    back_shaped = jnp.swapaxes(
        route_grad.reshape(exp_dev, blk_count, slot_count, model_width), 0, 1
    )
    returned = lax.all_to_all(
        back_shaped.reshape(blk_count, per_peer, model_width),
        "blk",
        split_axis=0,
        concat_axis=0,
        tiled=True,
    )
    by_route = returned.reshape(buffer_rows, model_width)[target].reshape(
        tok_dev, top_count, model_width
    )
    d_tokens = jnp.sum(by_route.astype(jnp.float32), axis=1).astype(jnp.bfloat16)
    term_gate = jnp.einsum("erd,erf->edf", inputs, grad_gate, preferred_element_type=jnp.float32)
    term_up = jnp.einsum("erd,erf->edf", inputs, grad_up, preferred_element_type=jnp.float32)
    term_down = jnp.einsum(
        "erf,erd->efd", scaled_hidden, cotangents, preferred_element_type=jnp.float32
    )
    sum_gate, sum_up, sum_down = (
        lax.psum_scatter(term_gate, "grp", scatter_dimension=1, tiled=True),
        lax.psum_scatter(term_up, "grp", scatter_dimension=1, tiled=True),
        lax.psum_scatter(term_down, "grp", scatter_dimension=2, tiled=True),
    )
    return (
        d_tokens,
        sum_gate.astype(jnp.bfloat16),
        sum_up.astype(jnp.bfloat16),
        sum_down.astype(jnp.bfloat16),
    )


def solution(mesh):
    return jax.shard_map(
        per_device,
        mesh=mesh,
        in_specs=(
            P(("grp", "blk"), None),
            P(("grp", "blk"), None),
            P(("grp", "blk"), None),
            P(("grp", "blk"), None),
            P(("grp", "blk"), None, None),
            P(("grp", "blk"), None, None),
            P("blk", None, None),
            P("blk", None, None),
            P("blk", None, None),
        ),
        out_specs=(
            P(("grp", "blk"), None),
            P("blk", "grp", None),
            P("blk", "grp", None),
            P("blk", None, "grp"),
        ),
        check_vma=False,
    )
```

profile of v0, /device:TPU:1, one launch (start us, length us, event | category | flops | bytes accessed | tf_op | source)
XLA Modules:
  0.0 719.1 jit_solution(11843196313732137014)
XLA Ops:
  19.3 5.4 gather_fusion
  25.5 11.0 %all-to-all-start = ((bf16[32,1,26]{2,1,0:T(2,128)(2,1)}), bf16[32,1,26]{2,1,0:T(2,128)(2,1)S(1)}, u32[]{:S(2)}, u32[]{:S(2)}) async-start(bf16[32,1,26]{2,1,0:T(2,128)(2,1)} %all_to_all.28), calls=%async_computation | async-start | bytes 32768 | tf_op jit(solution)/shard_map/all_to_all | solution.py:94
  43.0 6.2 gather_fusion.3
  58.9 6.2 gather_fusion.2
  72.5 47.5 %all_to_all.35 = bf16[32,26,704]{2,1,0:T(8,128)(2,1)} all-to-all(bf16[32,26,704]{2,1,0:T(8,128)(2,1)} %get-tuple-element.10), channel_id=1, replica_groups=mesh['grp'=8,'blk'=32] {'blk'}, dimensions={0} | all-to-all | bytes 2342912 | tf_op jit(solution)/shard_map/all_to_all | solution.py:87
  120.0 7.0 all-to-all-start.3
  132.0 4.9 gather.28
  146.7 5.8 broadcast_select_fusion
  152.5 13.0 %all-to-all-done.3 = bf16[32,26,704]{2,1,0:T(8,128)(2,1)} async-done(((bf16[32,26,704]{2,1,0:T(8,128)(2,1)}), bf16[32,26,704]{2,1,0:T(8,128)(2,1)}, u32[]{:S(2)}, u32[]{:S(2)}) %all-to-all-start.3) | async-done | bytes 1171488 | tf_op jit(solution)/shard_map/all_to_all | solution.py:80
  165.5 99.5 %all_to_all.36 = bf16[32,26,2048]{2,1,0:T(8,128)(2,1)} all-to-all(bf16[32,26,2048]{2,1,0:T(8,128)(2,1)} %get-tuple-element.7), channel_id=1, replica_groups=mesh['grp'=8,'blk'=32] {'blk'}, dimensions={0} | all-to-all | bytes 6815744 | tf_op jit(solution)/shard_map/all_to_all | solution.py:73
  265.0 6.7 all-to-all-start.5
  290.4 9.6 %multiply_convert_fusion.1 = (bf16[832,704]{0,1:T(8,128)(2,1)}, bf16[832,704]{0,1:T(8,128)(2,1)}) fusion(f32[832,704]{0,1:T(8,128)} %copy.37, f32[832]{0:T(1024)S(1)} %reshape.278, f32[832,704]{0,1:T(8,128)} %copy.35, bf16[832,2048]{1,0:T(8,128)(2,1)} %reshape.269, bf16[1,704,2048]{2,1,0:T(8,128)(2,1)} %param.17), kind=kOutput, calls=%fused_computation.20 | convolution fusion | flops 2407342080 | bytes 13323520 | tf_op jit(solution)/shard_map/erd,efd->erf/dot_general | solution.py:12
  299.9 66.5 %all-to-all-done.5 = bf16[32,26,2048]{2,1,0:T(8,128)(2,1)} async-done(((bf16[32,26,2048]{2,1,0:T(8,128)(2,1)}), bf16[32,26,2048]{2,1,0:T(8,128)(2,1)}, u32[]{:S(2)}, u32[]{:S(2)}) %all-to-all-start.5) | async-done | bytes 3407904 | tf_op jit(solution)/shard_map/all_to_all | solution.py:66
  371.3 8.0 %convolution_bitcast_fusion = f32[1,2048,704]{1,2,0:T(8,128)} fusion(bf16[832,704]{0,1:T(8,128)(2,1)} %get-tuple-element.4, bf16[832,2048]{1,0:T(8,128)(2,1)} %reshape.277), kind=kOutput, calls=%fused_computation.11 | convolution fusion | flops 2399141888 | bytes 10346496 | tf_op jit(solution)/shard_map/erd,erf->edf/dot_general | solution.py:128
  379.6 8.0 %convolution_bitcast_fusion.1 = f32[1,2048,704]{1,2,0:T(8,128)} fusion(bf16[832,704]{0,1:T(8,128)(2,1)} %get-tuple-element.5, bf16[832,2048]{1,0:T(8,128)(2,1)} %reshape.277), kind=kOutput, calls=%fused_computation.12 | convolution fusion | flops 2399141888 | bytes 10346496 | tf_op jit(solution)/shard_map/erd,erf->edf/dot_general | solution.py:127
  394.8 9.3 %convolution_bitcast_fusion.2 = f32[1,704,2048]{2,1,0:T(8,128)} fusion(bf16[832,2048]{1,0:T(8,128)(2,1)} %reshape.269, f32[1,832,1,1,1,1,704]{6,1,5,4,3,2,0:T(8,128)} %reshape.282, f32[1,832,1,1,1,1,704]{6,1,5,4,3,2,0:T(8,128)} %reshape.281, f32[832]{0:T(1024)S(1)} %reshape.278), kind=kOutput, calls=%fused_computation.13 | convolution fusion | flops 2403241984 | bytes 13864192 | tf_op jit(solution)/shard_map/erf,erd->efd/dot_general | solution.py:129
  413.1 5.0 reshape_transpose_reshape.2
  418.1 7.7 %all-to-all-start.4 = ((bf16[32,26,2048]{2,1,0:T(8,128)(2,1)}), bf16[32,26,2048]{2,1,0:T(8,128)(2,1)}, u32[]{:S(2)}, u32[]{:S(2)}) async-start(bf16[32,26,2048]{2,1,0:T(8,128)(2,1)} %reshape_transpose_reshape.2), calls=%async_computation.4 | async-start | bytes 8388608 | tf_op jit(solution)/shard_map/all_to_all | solution.py:116
  425.8 94.5 %all-to-all-done.4 = bf16[32,26,2048]{2,1,0:T(8,128)(2,1)} async-done(((bf16[32,26,2048]{2,1,0:T(8,128)(2,1)}), bf16[32,26,2048]{2,1,0:T(8,128)(2,1)}, u32[]{:S(2)}, u32[]{:S(2)}) %all-to-all-start.4) | async-done | bytes 3407904 | tf_op jit(solution)/shard_map/all_to_all | solution.py:116
  525.2 9.5 %gather_fusion.4 = bf16[768,2048]{1,0:T(8,128)(2,1)} fusion(bf16[832,2048]{1,0:T(8,128)(2,1)} %reshape.275, s32[1024]{0:T(1024)S(1)} %pad_clamp_fusion), kind=kCustom, calls=%fused_computation.4 | custom fusion | bytes 6294528 | tf_op jit(solution)/shard_map/gather | solution.py:123
  534.6 6.3 reshape.276
  540.9 5.8 reduce_sum.25
  548.7 58.9 %reduce-scatter.4.cloned.1.call-done = f32[1,256,704]{1,2,0:T(8,128)} async-done(((f32[1,2048,704]{1,2,0:T(8,128)}), f32[1,256,704]{1,2,0:T(8,128)}) %reduce-scatter.4.cloned.1.call-update) | async-done | bytes 720912 | tf_op jit(solution)/shard_map/reduce_scatter | solution.py:133
  609.4 101.0 %reduce-scatter.8.cloned.1.call-done = f32[1,704,256]{2,1,0:T(8,128)} async-done(((f32[1,704,2048]{2,1,0:T(8,128)}), f32[1,704,256]{2,1,0:T(8,128)}) %reduce-scatter.8.cloned.1.call-update) | async-done | bytes 720912 | tf_op jit(solution)/shard_map/reduce_scatter | solution.py:135
  (68 shorter events, 101.5 us)
Async XLA Ops:
  7.2 397.0 %copy-start = (bf16[1,2048,704]{1,2,0:T(8,128)(2,1)S(1)}, bf16[1,2048,704]{1,2,0:T(8,128)(2,1)}, u32[]{:S(2)}) copy-start(bf16[1,2048,704]{1,2,0:T(8,128)(2,1)} %param.15) | copy-start | bytes 8650756
  25.5 47.0 %all-to-all-start = ((bf16[32,1,26]{2,1,0:T(2,128)(2,1)}), bf16[32,1,26]{2,1,0:T(2,128)(2,1)S(1)}, u32[]{:S(2)}, u32[]{:S(2)}) async-start(bf16[32,1,26]{2,1,0:T(2,128)(2,1)} %all_to_all.28), calls=%async_computation | async-start | bytes 32768 | tf_op jit(solution)/shard_map/all_to_all | solution.py:94
  72.5 54.5 %copy-start.1 = (bf16[128,2048]{1,0:T(8,128)(2,1)S(1)}, bf16[128,2048]{1,0:T(8,128)(2,1)}, u32[]{:S(2)}) copy-start(bf16[128,2048]{1,0:T(8,128)(2,1)} %param.10) | copy-start | bytes 1572868
  120.0 45.5 %all-to-all-start.3 = ((bf16[32,26,704]{2,1,0:T(8,128)(2,1)}), bf16[32,26,704]{2,1,0:T(8,128)(2,1)}, u32[]{:S(2)}, u32[]{:S(2)}) async-start(bf16[32,26,704]{2,1,0:T(8,128)(2,1)} %get-tuple-element.11), calls=%async_computation.3 | async-start | bytes 3145728 | tf_op jit(solution)/shard_map/all_to_all | solution.py:80
  132.0 5.0 copy-start.2
  265.0 101.4 %all-to-all-start.5 = ((bf16[32,26,2048]{2,1,0:T(8,128)(2,1)}), bf16[32,26,2048]{2,1,0:T(8,128)(2,1)}, u32[]{:S(2)}, u32[]{:S(2)}) async-start(bf16[32,26,2048]{2,1,0:T(8,128)(2,1)} %get-tuple-element.6), calls=%async_computation.5 | async-start | bytes 8388608 | tf_op jit(solution)/shard_map/all_to_all | solution.py:66
  271.7 275.0 %reduce-scatter.6.cloned.1.call-start = ((), (), s32[]{:S(2)}) async-start(), calls=%async_computation.10 | async-start | bytes 6488064 | tf_op jit(solution)/shard_map/reduce_scatter | solution.py:134
  379.4 228.2 %reduce-scatter.4.cloned.1.call-start = ((), (), s32[]{:S(2)}) async-start(), calls=%async_computation.9 | async-start | bytes 6488064 | tf_op jit(solution)/shard_map/reduce_scatter | solution.py:133
  387.6 322.8 %reduce-scatter.8.cloned.1.call-start = ((), (), s32[]{:S(2)}) async-start(), calls=%async_computation.11 | async-start | bytes 6488064 | tf_op jit(solution)/shard_map/reduce_scatter | solution.py:135
  404.2 4.4 copy-start.3
  404.2 4.4 copy-start.4
  418.1 102.2 %all-to-all-start.4 = ((bf16[32,26,2048]{2,1,0:T(8,128)(2,1)}), bf16[32,26,2048]{2,1,0:T(8,128)(2,1)}, u32[]{:S(2)}, u32[]{:S(2)}) async-start(bf16[32,26,2048]{2,1,0:T(8,128)(2,1)} %reshape_transpose_reshape.2), calls=%async_computation.4 | async-start | bytes 8388608 | tf_op jit(solution)/shard_map/all_to_all | solution.py:116
Sparse Core Ops, SparseCore 0:
  379.5 126.9 reduce-scatter.5
  510.7 96.7 reduce-scatter.3
  611.7 98.6 reduce-scatter.7
where the time goes:
time: 729 us; the launch traced here: 719 us
  waiting for transfers between devices  334 us (46%)
  blocking collectives  147 us (20%)
  local copies, waits for them, and re-layouts  123 us (17%)
  matrix products  43.8 us (6%)
  starting transfers between devices  32.7 us (4%)
  other arithmetic  23.9 us (3%)
  between operations  14.2 us (2%)
    reduce_scatter x1, waiting for transfers between devices, per_device(): lax.psum_scatter(term_down, 'grp', scatter_dimension=2, tiled=True)  101 us
    all_to_all x1, blocking collectives, per_device(): lax.all_to_all(send_grads.reshape(blk_count, per_peer, model_width), 'blk...  99.5 us
    all_to_all x1, waiting for transfers between devices, per_device(): lax.all_to_all(back_shaped.reshape(blk_count, per_peer, model_width), 'bl...  94.5 us
    all_to_all x1, waiting for transfers between devices, per_device(): lax.all_to_all(send_inputs.reshape(blk_count, per_peer, model_width), 'bl...  66.5 us
    reduce_scatter x1, waiting for transfers between devices, per_device(): lax.psum_scatter(term_gate, 'grp', scatter_dimension=1, tiled=True)  58.9 us
    all_to_all x1, blocking collectives, per_device(): lax.all_to_all(send_up_pre.reshape(blk_count, per_peer, ffw_width), 'blk'...  47.5 us
    gather x9, local copies, waits for them, and re-layouts, pick(): taken = table[rows]  44.4 us
  transfers between devices with their start and end apart: 7, of which 5 were waited for; matrix products, arithmetic and copies ran while one was open for 22% of the time, Pallas kernels for 0%

commit v1 on v0

v1 whole, which is shorter than its diff:
```python
import jax
import jax.numpy as jnp
from jax import lax
from jax.experimental import pallas as pl
from jax.experimental.pallas import tpu as pltpu
from jax.sharding import PartitionSpec as P

MESH = pl.DeviceIdType.MESH
RING = 8
NEAR = 4
HOPS = RING // 2
PAD = 32


def place():
    me = lax.axis_index("blk")
    return me // (2 * RING) * 2 + lax.rem(me, 2), lax.rem(me // 2, RING)


def at(near, z):
    return near // 2 * (2 * RING) + z * 2 + lax.rem(near, 2)


def wrap(z):
    return lax.rem(z + RING, RING)


def greet(peers):
    barrier = pltpu.get_barrier_semaphore()
    for peer in peers:
        pl.semaphore_signal(barrier, inc=1, device_id=peer, device_id_type=MESH)
    return barrier


def remote(src, dst, send, recv, peer):
    return pltpu.make_async_remote_copy(
        src_ref=src, dst_ref=dst, send_sem=send, recv_sem=recv, device_id=peer, device_id_type=MESH
    )


def spread_kernel(
    d_ref, t_ref, g_ref, pre_ref, rd_ref, rt_ref, rpre_ref, rg_ref,
    ring_d, ring_t, pick_d, pick_t, ring_s, ring_r, near_s, near_r, near_l, g_s, g_r, pre_s, pre_r, own_sem,
):
    near, z = place()
    me = lax.axis_index("blk")
    count = 2 * 2 * RING
    barrier = pltpu.get_barrier_semaphore()

    def hello(k, carry):
        pl.semaphore_signal(
            barrier, inc=1, device_id={"blk": lax.rem(me + k, count)}, device_id_type=MESH
        )
        return carry

    lax.fori_loop(1, count, hello, 0)
    pl.semaphore_wait(barrier, count - 1)

    own_refs, rings = (d_ref, t_ref), (ring_d, ring_t)
    picks, lands = (pick_d, pick_t), (rd_ref, rt_ref)
    half = d_ref.shape[0] // 2

    def hop(a, way, k):
        step = 1 if way == 0 else -1
        source = wrap(z - step * k)
        src = own_refs[a] if k == 0 else rings[a].at[source]
        dst = rings[a].at[source]
        if k == HOPS - 1:
            src = src.at[pl.ds(way * half, half)]
            dst = dst.at[pl.ds(way * half, half)]
        return remote(
            src, dst, ring_s.at[a, way, k], ring_r.at[a, way, k], {"blk": at(near, wrap(z + step))}
        )

    def g_copy(k):
        to = wrap(z + k)
        return remote(g_ref.at[to], rg_ref.at[z], g_s.at[k], g_r.at[k], {"blk": at(near, to)})

    def pre_copy(k):
        to = lax.rem(me + k, count)
        return remote(pre_ref.at[to], rpre_ref.at[near, z], pre_s.at[k], pre_r.at[k], {"blk": to})

    for a in range(2):
        for way in range(2):
            hop(a, way, 0).start()
    for k in range(1, RING):
        g_copy(k).start()
    own_g = pltpu.make_async_copy(g_ref.at[z], rg_ref.at[z], own_sem.at[0])
    own_g.start()
    own_pre = pltpu.make_async_copy(pre_ref.at[me], rpre_ref.at[near, z], own_sem.at[1])
    own_pre.start()

    def pre_start(k, carry):
        pre_copy(k).start()
        return carry

    lax.fori_loop(1, count, pre_start, 0)

    def near_copy(a, source, number, j):
        to = lax.rem(near + j, NEAR)
        src = picks[a].at[source, to]
        if j == 0:
            return pltpu.make_async_copy(src, lands[a].at[near, source], near_l.at[a, number])
        return remote(
            src, lands[a].at[near, source], near_s.at[a, number, j], near_r.at[a, number, j],
            {"blk": at(to, z)},
        )

    def gather(a, source, number):
        rows = own_refs[a][...] if number == 0 else rings[a][source]
        taken = jnp.dot(rg_ref[source], rows, preferred_element_type=jnp.float32)
        picks[a][source] = taken.astype(jnp.bfloat16).reshape(NEAR, PAD, taken.shape[1])
        for j in (1, 2, 3, 0):
            near_copy(a, source, number, j).start()

    own_g.wait()
    for a in range(2):
        gather(a, z, 0)
    for k in range(1, RING):
        g_copy(k).wait()
    for k in range(HOPS):
        for a in range(2):
            for way in range(2):
                hop(a, way, k).wait_recv()
                if k + 1 < HOPS:
                    hop(a, way, k + 1).start()
            if k + 1 < HOPS:
                gather(a, wrap(z - k - 1), 2 * k + 1)
                gather(a, wrap(z + k + 1), 2 * k + 2)
            else:
                gather(a, wrap(z + HOPS), 2 * k + 1)

    own_pre.wait()

    def pre_wait(k, carry):
        pre_copy(k).wait()
        return carry

    lax.fori_loop(1, count, pre_wait, 0)
    for a in range(2):
        for way in range(2):
            for k in range(HOPS):
                hop(a, way, k).wait_send()
        for number in range(RING):
            offset = (number + 1) // 2
            source = wrap(z - offset if number % 2 else z + offset)
            for j in range(NEAR):
                near_copy(a, source, number, j).wait()


def fold_kernel(
    ret_ref, g_ref, w_ref, out_ref, rw_ref,
    land, part, ring, near_s, near_r, near_l, ring_s, ring_r, w_s, w_r,
):
    near, z = place()
    grp = lax.axis_index("grp")
    groups = lax.axis_size("grp")
    width = w_ref.shape[2] // groups
    barrier = greet(
        [{"grp": lax.rem(grp + j, groups)} for j in range(1, groups)]
        + [{"blk": at(lax.rem(near + j, NEAR), z)} for j in range(1, NEAR)]
        + [{"blk": at(near, wrap(z + step))} for step in (1, -1)]
    )
    pl.semaphore_wait(barrier, groups + NEAR)

    def near_copy(number, j):
        offset = (number + 1) // 2
        source = wrap(z - offset if number % 2 else z + offset)
        to = lax.rem(near + j, NEAR)
        src, dst = ret_ref.at[to, source], land.at[source, near]
        if j == 0:
            return pltpu.make_async_copy(src, dst, near_l.at[number])
        return remote(src, dst, near_s.at[number, j], near_r.at[number, j], {"blk": at(to, z)})

    def w_copy(j):
        to = lax.rem(grp + j, groups)
        cols = pl.ds(pl.multiple_of(to * width, width), width)
        return remote(w_ref.at[:, :, cols], rw_ref.at[j - 1], w_s.at[j], w_r.at[j], {"grp": to})

    for number in reversed(range(RING)):
        for j in (1, 2, 3, 0):
            near_copy(number, j).start()
    for j in range(1, groups):
        w_copy(j).start()

    half = out_ref.shape[0] // 2

    def hop(way, k):
        step = 1 if way == 0 else -1
        src, dst = part.at[way, k], ring.at[way, k]
        if k == 0:
            src, dst = src.at[pl.ds(0, half)], dst.at[pl.ds(0, half)]
        return remote(src, dst, ring_s.at[way, k], ring_r.at[way, k], {"blk": at(near, wrap(z + step))})

    def scattered(number):
        offset = (number + 1) // 2
        source = wrap(z - offset if number % 2 else z + offset)
        for j in range(NEAR):
            near_copy(number, j).wait()
        rows = land[source].reshape(NEAR * PAD, out_ref.shape[1])
        return jnp.dot(g_ref[source], rows, preferred_element_type=jnp.float32)

    far = scattered(RING - 1).astype(jnp.bfloat16)
    for way in range(2):
        part[way, 0, 0:half] = far[way * half : (way + 1) * half]
        hop(way, 0).start()
    for k in range(1, HOPS):
        for way in range(2):
            offset = HOPS - k
            own = scattered(2 * offset if way == 0 else 2 * offset - 1)
            hop(way, k - 1).wait_recv()
            if k == 1:
                low = ring[way, 0, 0:half].astype(jnp.float32)
                rows = slice(way * half, (way + 1) * half)
                part[way, k] = own.astype(jnp.bfloat16)
                part[way, k, rows] = (own[rows] + low).astype(jnp.bfloat16)
            else:
                part[way, k] = (own + ring[way, k - 1].astype(jnp.float32)).astype(jnp.bfloat16)
            hop(way, k).start()
    own = scattered(0)
    for way in range(2):
        hop(way, HOPS - 1).wait_recv()
        own = own + ring[way, HOPS - 1].astype(jnp.float32)
    out_ref[...] = own.astype(jnp.bfloat16)
    for way in range(2):
        for k in range(HOPS):
            hop(way, k).wait_send()
    for j in range(1, groups):
        w_copy(j).wait()


def spread(d_out, tokens, onehot, pre):
    rows, width = d_out.shape
    bf16, dma = jnp.bfloat16, pltpu.SemaphoreType.DMA
    vmem, anywhere = pl.BlockSpec(memory_space=pltpu.VMEM), pl.BlockSpec(memory_space=pl.ANY)
    landed = jax.ShapeDtypeStruct((NEAR, RING, PAD, width), bf16)
    return pl.pallas_call(
        spread_kernel,
        out_shape=(
            landed,
            landed,
            jax.ShapeDtypeStruct((NEAR, RING) + pre.shape[1:], bf16),
            jax.ShapeDtypeStruct(onehot.shape, bf16),
        ),
        in_specs=[vmem, vmem, vmem, anywhere],
        out_specs=(vmem, vmem, anywhere, vmem),
        scratch_shapes=[
            pltpu.VMEM((RING, rows, width), bf16),
            pltpu.VMEM((RING, rows, width), bf16),
            pltpu.VMEM((RING, NEAR, PAD, width), bf16),
            pltpu.VMEM((RING, NEAR, PAD, width), bf16),
            dma((2, 2, HOPS)),
            dma((2, 2, HOPS)),
            dma((2, RING, NEAR)),
            dma((2, RING, NEAR)),
            dma((2, RING)),
            dma((RING,)),
            dma((RING,)),
            dma((NEAR * RING,)),
            dma((NEAR * RING,)),
            dma((2,)),
        ],
        compiler_params=pltpu.CompilerParams(
            collective_id=0, has_side_effects=True, vmem_limit_bytes=48 << 20
        ),
        name="spread",
    )(d_out, tokens, onehot, pre)


def fold(ret, onehot_t, terms):
    width = ret.shape[-1]
    rows = onehot_t.shape[1]
    bf16, dma = jnp.bfloat16, pltpu.SemaphoreType.DMA
    vmem, anywhere = pl.BlockSpec(memory_space=pltpu.VMEM), pl.BlockSpec(memory_space=pl.ANY)
    groups = lax.axis_size("grp")
    return pl.pallas_call(
        fold_kernel,
        out_shape=(
            jax.ShapeDtypeStruct((rows, width), bf16),
            jax.ShapeDtypeStruct((groups - 1,) + terms.shape[:2] + (terms.shape[2] // groups,), bf16),
        ),
        in_specs=[vmem, vmem, anywhere],
        out_specs=(vmem, anywhere),
        scratch_shapes=[
            pltpu.VMEM((RING, NEAR, PAD, width), bf16),
            pltpu.VMEM((2, HOPS, rows, width), bf16),
            pltpu.VMEM((2, HOPS, rows, width), bf16),
            dma((RING, NEAR)),
            dma((RING, NEAR)),
            dma((RING,)),
            dma((2, HOPS)),
            dma((2, HOPS)),
            dma((groups,)),
            dma((groups,)),
        ],
        compiler_params=pltpu.CompilerParams(
            collective_id=1, has_side_effects=True, vmem_limit_bytes=48 << 20
        ),
        name="fold",
    )(ret, onehot_t, terms)


def per_device(
    tokens, d_out, expert_ids, gate_values, saved_gate_pre, saved_up_pre, w_gate, w_up, w_down
):
    bf16, f32 = jnp.bfloat16, jnp.float32
    rows, width = tokens.shape
    ffw = saved_gate_pre.shape[2]
    experts = NEAR * RING
    chosen = expert_ids[:, :, None] == jnp.arange(experts, dtype=jnp.int32)[None, None, :]
    hit = jnp.any(chosen, axis=1)
    before = jnp.tril(jnp.ones((rows, rows), bf16), -1)
    rank = jnp.dot(before, hit.astype(bf16), preferred_element_type=f32).astype(jnp.int32)
    slot = jnp.where(hit, rank, PAD).T
    onehot = (slot[:, None, :] == jnp.arange(PAD, dtype=jnp.int32)[None, :, None])
    by_z = onehot.astype(bf16).reshape(2, RING, 2, PAD, rows)
    by_z = jnp.transpose(by_z, (1, 0, 2, 3, 4)).reshape(RING, NEAR * PAD, rows)
    route = (onehot[None] & chosen.transpose(1, 2, 0)[:, :, None, :]).astype(bf16)
    route = route.reshape(-1, experts * PAD, rows)
    picked = [
        jnp.einsum("kst,tkf->sf", route, table, preferred_element_type=bf16)
        for table in (saved_gate_pre, saved_up_pre)
    ]
    gate_of = jnp.sum(jnp.where(chosen, gate_values.astype(f32)[:, :, None], 0.0), axis=1).T
    gate_slot = jnp.sum(jnp.where(onehot, gate_of[:, None, :], 0.0), axis=2)
    pre = jnp.concatenate(picked, axis=1).reshape(experts, PAD, 2 * ffw)
    slots = 13 * rows // (2 * experts)
    pre = pre + jnp.pad(
        gate_slot.astype(bf16)[:, None, :], ((0, 0), (slots, PAD - slots - 1), (0, 2 * ffw - PAD))
    )

    recv_d, recv_t, recv_pre, recv_g = spread(d_out, tokens, by_z, pre)

    cot = recv_d.reshape(experts * PAD, width)
    inputs = recv_t.reshape(experts * PAD, width)
    weights = recv_pre[:, :, slots, :PAD].astype(f32).reshape(experts * PAD, 1)
    recv_pre = recv_pre.reshape(experts * PAD, 2 * ffw)
    gate_pre = recv_pre[:, :ffw].astype(f32)
    up_pre = recv_pre[:, ffw:].astype(f32)
    sig = jax.nn.sigmoid(gate_pre)
    active = gate_pre * sig
    hidden = (weights * active * up_pre).astype(bf16)
    back = weights * jnp.einsum("rd,fd->rf", cot, w_down[0], preferred_element_type=f32)
    grad_gate = (back * up_pre * sig * (1.0 + gate_pre * (1.0 - sig))).astype(bf16)
    grad_up = (back * active).astype(bf16)
    ret = (
        jnp.einsum("rf,df->rd", grad_gate, w_gate[0], preferred_element_type=f32)
        + jnp.einsum("rf,df->rd", grad_up, w_up[0], preferred_element_type=f32)
    ).astype(bf16)
    terms = jnp.stack(
        [
            jnp.einsum("rf,rd->fd", left, right, preferred_element_type=f32).astype(bf16)
            for left, right in ((grad_gate, inputs), (grad_up, inputs), (hidden, cot))
        ]
    )

    d_tokens, got = fold(
        ret.reshape(NEAR, RING, PAD, width), jnp.swapaxes(recv_g, 1, 2), terms
    )
    mine = lax.dynamic_slice_in_dim(
        terms, lax.axis_index("grp") * got.shape[3], got.shape[3], axis=2
    )
    sums = (jnp.sum(got.astype(f32), axis=0) + mine.astype(f32)).astype(bf16)
    return (
        d_tokens,
        jnp.swapaxes(sums[0], 0, 1)[None],
        jnp.swapaxes(sums[1], 0, 1)[None],
        sums[2][None],
    )


def solution(mesh):
    rows = P(("grp", "blk"), None)
    return jax.shard_map(
        per_device,
        mesh=mesh,
        in_specs=(
            rows,
            rows,
            rows,
            rows,
            P(("grp", "blk"), None, None),
            P(("grp", "blk"), None, None),
            P("blk", None, None),
            P("blk", None, None),
            P("blk", None, None),
        ),
        out_specs=(rows, P("blk", "grp", None), P("blk", "grp", None), P("blk", None, "grp")),
        check_vma=False,
    )
```

time: 729 us -> 436 us (0.60)
  Pallas kernels: 0 us -> 359 us
  waiting for transfers between devices: 334 us -> 0 us
  blocking collectives: 147 us -> 0 us
  local copies, waits for them, and re-layouts: 123 us -> 17.9 us
  starting transfers between devices: 32.7 us -> 0 us
  between operations: 14.2 us -> 0.93 us
  matrix products: 43.8 us -> 31.9 us
    pallas_call x0 -> x2, Pallas kernels: none -> 359 us  [the longest x1 181 us: fold(): pl.pallas_call(fold_kernel, out_shape=(jax.ShapeDtypeStruct((rows, width)...]
    all_to_all x4 -> x0, waiting for transfers between devices: 174 us -> none  [the longest x1 94.5 us: per_device(): lax.all_to_all(back_shaped.reshape(blk_count, per_peer, model_width), 'bl...]
    reduce_scatter x3 -> x0, waiting for transfers between devices: 160 us -> none  [the longest x1 101 us: per_device(): lax.psum_scatter(term_down, 'grp', scatter_dimension=2, tiled=True)]
    all_to_all x2 -> x0, blocking collectives: 147 us -> none  [the longest x1 99.5 us: per_device(): lax.all_to_all(send_grads.reshape(blk_count, per_peer, model_width), 'blk...]
    gather x10 -> x0, local copies, waits for them, and re-layouts: 53.9 us -> none  [the longest x9 44.4 us: pick(): taken = table[rows]]
    all_to_all x4 -> x0, starting transfers between devices: 32.4 us -> none  [the longest x1 11 us: per_device(): lax.all_to_all(send_gate.reshape(blk_count, per_peer), 'blk', split_axis=...]
    convert_element_type x7 -> x2, local copies, waits for them, and re-layouts: 20.9 us -> 0.09 us  [the longest x1 0.07 us: per_device(): weights = recv_pre[:, :, slots, :PAD].astype(f32).reshape(experts * PAD, 1)]
    reshape x5 -> x0, local copies, waits for them, and re-layouts: 18 us -> none  [the longest x2 11.2 us: per_device(): returned.reshape(buffer_rows, model_width)[target]]
  transfers between devices with their start and end apart: 7 -> 0, of which waited for: 5 -> 0; matrix products, arithmetic and copies ran while one was open for 22% -> 0% of each run, Pallas kernels for 0% -> 0%
where the time goes in v1:
time: 436 us; the launch traced here: 431 us
  Pallas kernels  359 us (82%)
  matrix products  31.9 us (7%)
  other arithmetic  21 us (5%)
  local copies, waits for them, and re-layouts  17.9 us (4%)
    pallas_call x1, Pallas kernels, fold(): pl.pallas_call(fold_kernel, out_shape=(jax.ShapeDtypeStruct((rows, width)...  181 us
    pallas_call x1, Pallas kernels, spread(): pl.pallas_call(spread_kernel, out_shape=(landed, landed, jax.ShapeDtypeSt...  177 us
    dot_general x3, matrix products, per_device(): jnp.einsum('rf,rd->fd', left, right, preferred_element_type=f32)  10.6 us
    unnamed x37, local copies, waits for them, and re-layouts  9.23 us

profile of v1, /device:TPU:1, one launch (start us, length us, event | category | flops | bytes accessed | tf_op | source)
XLA Modules:
  0.0 430.7 jit_solution(9689145524282754856)
XLA Ops:
  0.6 0.9 fusion.20
  3.1 2.7 convolution_bitcast_fusion
  5.8 1.3 convolution_bitcast_fusion.1
  7.1 1.9 pad_maximum_fusion.1
  9.0 4.6 %copy.29 = bf16[1024,1408]{1,0:T(8,128)(2,1)} copy(bf16[1024,1408]{0,1:T(8,128)(2,1)} %pad_maximum_fusion.1) | data formatting | bytes 5767168 | tf_op jit(solution)/shard_map/concatenate | solution.py:326
  13.9 3.7 pad_add_fusion.pre_ref
  17.9 1.0 copy-done.6
  18.9 177.4 %spread.1 = (bf16[4,8,32,2048]{3,2,1,0:T(8,128)(2,1)}, bf16[4,8,32,2048]{3,2,1,0:T(8,128)(2,1)}, bf16[4,8,32,1408]{3,2,1,0:T(8,128)(2,1)S(1)}, bf16[8,128,128]{2,1,0:T(8,128)(2,1)S(1)}) custom-call(bf16[128,2048]{1,0:T(8,128)(2,1)S(1)} %copy-done.5, bf16[128,2048]{1,0:T(8,128)(2,1)S(1)} %copy-done.6, bf16[8,128,128]{2,1,0:T(8,128)(2,1)S(1)} %fusion.19.g_ref, ...), custom_call_target="tpu_custom_call" | custom-call | tf_op jit(solution)/shard_map/spread/pallas_call | solution.py:237
  196.3 2.7 fusion.29
  199.0 2.6 copy.34
  201.6 2.6 copy.35
  204.2 0.9 convert_reduce_fusion.1
  205.1 8.2 %multiply_convert_fusion = (bf16[1024,704]{0,1:T(8,128)(2,1)S(1)}, bf16[1024,704]{0,1:T(8,128)(2,1)S(1)}) fusion(f32[1024]{0:T(1024)S(1)} %reshape.68, bf16[1024,704]{0,1:T(8,128)(2,1)} %copy.35, bf16[1024,704]{0,1:T(8,128)(2,1)} %copy.34, bf16[1024,2048]{1,0:T(8,128)(2,1)} %bitcast.78, bf16[1,704,2048]{2,1,0:T(8,128)(2,1)} %param.17), kind=kOutput, calls=%fused_computation.29 | convolution fusion | flops 2964324352 | bytes 12849152 | tf_op jit(solution)/shard_map/rd,fd->rf/dot_general | solution.py:343
  213.4 3.4 fusion
  216.8 3.6 fusion.1
  220.4 3.7 fusion.2
  224.1 4.0 pad_maximum_fusion.w_ref
  228.1 3.5 fusion.12
  231.6 5.4 %add_convert_fusion = bf16[1024,2048]{1,0:T(8,128)(2,1)} fusion(f32[1024,2048]{1,0:T(8,128)S(1)} %fusion.12, bf16[1024,704]{0,1:T(8,128)(2,1)S(1)} %get-tuple-element.16, bf16[1,2048,704]{1,2,0:T(8,128)(2,1)S(1)} %copy-done.15), kind=kOutput, calls=%fused_computation.2 | convolution fusion | flops 2956984320 | bytes 16908288 | tf_op jit(solution)/shard_map/rf,df->rd/dot_general | solution.py:348
  237.2 2.2 copy-done.1
  239.4 181.5 %fold.1 = (bf16[128,2048]{1,0:T(8,128)(2,1)S(1)}, bf16[7,3,704,256]{3,2,1,0:T(8,128)(2,1)}) custom-call(bf16[4,8,32,2048]{3,2,1,0:T(8,128)(2,1)S(1)} %bitcast.70, bf16[8,128,128]{2,1,0:T(8,128)(2,1)S(1)} %bitcast.72, bf16[3,704,2048]{2,1,0:T(8,128)(2,1)} %pad_maximum_fusion.w_ref), custom_call_target="tpu_custom_call" | custom-call | tf_op jit(solution)/shard_map/fold/pallas_call | solution.py:276
  420.9 5.8 %convert_reduce_fusion = f32[3,704,256]{2,1,0:T(8,128)} fusion(bf16[7,3,704,256]{3,2,1,0:T(8,128)(2,1)} %get-tuple-element.15), kind=kLoop, calls=%fused_computation | loop fusion | flops 7028736 | bytes 9732096 | tf_op jit(solution)/shard_map/reduce_sum | solution.py:363
  426.7 2.2 add_convert_fusion.1
  428.9 1.0 fusion.30
  (49 shorter events, 3.2 us)
Async XLA Ops:
  0.6 227.4 %copy-start = (bf16[1,2048,704]{1,2,0:T(8,128)(2,1)S(1)}, bf16[1,2048,704]{1,2,0:T(8,128)(2,1)}, u32[]{:S(2)}) copy-start(bf16[1,2048,704]{1,2,0:T(8,128)(2,1)} %param.15) | copy-start | bytes 8650756
  3.1 2.7 copy-start.16
  9.0 4.6 %copy-start.12 = (bf16[128,6]{0,1:T(8,128)(2,1)S(1)}, bf16[128,6]{0,1:T(8,128)(2,1)}, u32[]{:S(2)}) copy-start(bf16[128,6]{0,1:T(8,128)(2,1)} %param.12) | copy-start | bytes 4612
  9.0 4.6 %copy-start.11 = (s32[128,6]{0,1:T(8,128)S(1)}, s32[128,6]{0,1:T(8,128)}, u32[]{:S(2)}) copy-start(s32[128,6]{0,1:T(8,128)} %param.11) | copy-start | bytes 9220
  13.9 4.0 copy-start.5
  17.9 1.0 copy-start.6
  196.3 2.7 copy-start.2
  196.3 2.7 copy-start.7
  205.1 8.2 %copy-start.14 = (bf16[4,8,32,2048]{3,2,1,0:T(8,128)(2,1)S(1)}, bf16[4,8,32,2048]{3,2,1,0:T(8,128)(2,1)}, u32[]{:S(2)}) copy-start(bf16[4,8,32,2048]{3,2,1,0:T(8,128)(2,1)} %get-tuple-element.13) | copy-start | bytes 12582916
  216.7 3.6 copy-start.9
  216.7 3.6 copy-start.10
  216.7 3.6 copy-start.13
  228.1 3.5 copy-start.15
  231.6 5.4 %copy-start.8 = (bf16[8,128,128]{2,1,0:T(8,128)(2,1)S(1)}, bf16[8,128,128]{2,1,0:T(8,128)(2,1)}, u32[]{:S(2)}) copy-start(bf16[8,128,128]{2,1,0:T(8,128)(2,1)} %copy-done.7) | copy-start | bytes 786436
  237.2 2.2 copy-start.1
  420.9 5.8 %copy-start.3 = (bf16[128,2048]{1,0:T(8,128)(2,1)}, bf16[128,2048]{1,0:T(8,128)(2,1)S(1)}, u32[]{:S(2)}) copy-start(bf16[128,2048]{1,0:T(8,128)(2,1)S(1)} %get-tuple-element.27) | copy-start | bytes 1572868
  426.7 3.2 copy-start.4

commit v2 on v1

--- a/solution.py
+++ b/solution.py
@@ -10,6 +10,7 @@
 NEAR = 4
 HOPS = RING // 2
 PAD = 32
+SIDE = 4
 
 
 def place():
@@ -23,6 +24,10 @@
 
 def wrap(z):
     return lax.rem(z + RING, RING)
+
+
+def turn(y):
+    return lax.rem(y + 2 * SIDE, SIDE)
 
 
 def greet(peers):
@@ -149,19 +154,22 @@
 
 
 def fold_kernel(
-    ret_ref, g_ref, w_ref, out_ref, rw_ref,
-    land, part, ring, near_s, near_r, near_l, ring_s, ring_r, w_s, w_r,
+    ret_ref, g_ref, wg_ref, wu_ref, wd_ref, out_ref, sg_ref, su_ref, sd_ref,
+    land, part, ring, own_w, acc, cross, near_s, near_r, near_l, ring_s, ring_r, own_sem, w_s, w_r, x_s, x_r,
 ):
     near, z = place()
     grp = lax.axis_index("grp")
-    groups = lax.axis_size("grp")
-    width = w_ref.shape[2] // groups
+    side, y = grp // SIDE, lax.rem(grp, SIDE)
+    other = 1 - side
+    terms, sums = (wg_ref, wu_ref, wd_ref), (sg_ref, su_ref, sd_ref)
+    width = sg_ref.shape[1]
     barrier = greet(
-        [{"grp": lax.rem(grp + j, groups)} for j in range(1, groups)]
+        [{"grp": side * SIDE + turn(y + step)} for step in (1, -1)]
+        + [{"grp": other * SIDE + y}]
         + [{"blk": at(lax.rem(near + j, NEAR), z)} for j in range(1, NEAR)]
         + [{"blk": at(near, wrap(z + step))} for step in (1, -1)]
     )
-    pl.semaphore_wait(barrier, groups + NEAR)
+    pl.semaphore_wait(barrier, 5 + NEAR - 1)
 
     def near_copy(number, j):
         offset = (number + 1) // 2
@@ -172,16 +180,44 @@
             return pltpu.make_async_copy(src, dst, near_l.at[number])
         return remote(src, dst, near_s.at[number, j], near_r.at[number, j], {"blk": at(to, z)})
 
-    def w_copy(j):
-        to = lax.rem(grp + j, groups)
-        cols = pl.ds(pl.multiple_of(to * width, width), width)
-        return remote(w_ref.at[:, :, cols], rw_ref.at[j - 1], w_s.at[j], w_r.at[j], {"grp": to})
-
+    def cols(way, to):
+        start = ((other if way == 0 else side) * SIDE + to) * width
+        return pl.ds(pl.multiple_of(start, width), width)
+
+    def w_hop(way, k, t):
+        step = 1 if way == 0 else -1
+        src = terms[t].at[:, cols(way, turn(y - step))] if k == 0 else acc.at[way, k - 1, t]
+        return remote(
+            src, acc.at[way, k, t], w_s.at[way, k, t], w_r.at[way, k, t],
+            {"grp": side * SIDE + turn(y + step)},
+        )
+
+    def x_copy(t):
+        return remote(acc.at[0, SIDE - 2, t], cross.at[t], x_s.at[t], x_r.at[t], {"grp": other * SIDE + y})
+
+    def own_copy(t):
+        return pltpu.make_async_copy(terms[t], own_w.at[t], own_sem.at[t])
+
+    def w_sum(way, k, t):
+        step = 1 if way == 0 else -1
+        w_hop(way, k, t).wait_recv()
+        own = own_w[t, :, cols(way, turn(y - step * (k + 2)))]
+        return acc[way, k, t].astype(jnp.float32) + own.astype(jnp.float32)
+
+    def w_turn(k):
+        for t in range(3):
+            for way in range(2):
+                acc[way, k, t] = w_sum(way, k, t).astype(jnp.bfloat16)
+                w_hop(way, k + 1, t).start()
+
+    for t in range(3):
+        for way in range(2):
+            w_hop(way, 0, t).start()
     for number in reversed(range(RING)):
         for j in (1, 2, 3, 0):
             near_copy(number, j).start()
-    for j in range(1, groups):
-        w_copy(j).start()
+    for t in range(3):
+        own_copy(t).start()
 
     half = out_ref.shape[0] // 2
 
@@ -204,6 +240,8 @@
     for way in range(2):
         part[way, 0, 0:half] = far[way * half : (way + 1) * half]
         hop(way, 0).start()
+    for t in range(3):
+        own_copy(t).wait()
     for k in range(1, HOPS):
         for way in range(2):
             offset = HOPS - k
@@ -217,16 +255,29 @@
             else:
                 part[way, k] = (own + ring[way, k - 1].astype(jnp.float32)).astype(jnp.bfloat16)
             hop(way, k).start()
+        if k == 1:
+            w_turn(0)
+    w_turn(1)
     own = scattered(0)
     for way in range(2):
         hop(way, HOPS - 1).wait_recv()
         own = own + ring[way, HOPS - 1].astype(jnp.float32)
     out_ref[...] = own.astype(jnp.bfloat16)
+    for t in range(3):
+        acc[0, SIDE - 2, t] = w_sum(0, SIDE - 2, t).astype(jnp.bfloat16)
+        x_copy(t).start()
+    for t in range(3):
+        mine = w_sum(1, SIDE - 2, t)
+        x_copy(t).wait_recv()
+        sums[t][...] = (mine + cross[t].astype(jnp.float32)).astype(jnp.bfloat16)
     for way in range(2):
         for k in range(HOPS):
             hop(way, k).wait_send()
-    for j in range(1, groups):
-        w_copy(j).wait()
+        for k in range(SIDE - 1):
+            for t in range(3):
+                w_hop(way, k, t).wait_send()
+    for t in range(3):
+        x_copy(t).wait_send()
 
 
 def spread(d_out, tokens, onehot, pre):
@@ -272,32 +323,36 @@
     rows = onehot_t.shape[1]
     bf16, dma = jnp.bfloat16, pltpu.SemaphoreType.DMA
     vmem, anywhere = pl.BlockSpec(memory_space=pltpu.VMEM), pl.BlockSpec(memory_space=pl.ANY)
-    groups = lax.axis_size("grp")
+    ffw = terms[0].shape[0]
+    share = (ffw, width // lax.axis_size("grp"))
     return pl.pallas_call(
         fold_kernel,
-        out_shape=(
-            jax.ShapeDtypeStruct((rows, width), bf16),
-            jax.ShapeDtypeStruct((groups - 1,) + terms.shape[:2] + (terms.shape[2] // groups,), bf16),
-        ),
-        in_specs=[vmem, vmem, anywhere],
-        out_specs=(vmem, anywhere),
+        out_shape=(jax.ShapeDtypeStruct((rows, width), bf16),) + (jax.ShapeDtypeStruct(share, bf16),) * 3,
+        in_specs=[vmem, vmem, anywhere, anywhere, anywhere],
+        out_specs=(vmem,) * 4,
         scratch_shapes=[
             pltpu.VMEM((RING, NEAR, PAD, width), bf16),
             pltpu.VMEM((2, HOPS, rows, width), bf16),
             pltpu.VMEM((2, HOPS, rows, width), bf16),
+            pltpu.VMEM((3, ffw, width), bf16),
+            pltpu.VMEM((2, SIDE - 1, 3) + share, bf16),
+            pltpu.VMEM((3,) + share, bf16),
             dma((RING, NEAR)),
             dma((RING, NEAR)),
             dma((RING,)),
             dma((2, HOPS)),
             dma((2, HOPS)),
-            dma((groups,)),
-            dma((groups,)),
+            dma((3,)),
+            dma((2, SIDE - 1, 3)),
+            dma((2, SIDE - 1, 3)),
+            dma((3,)),
+            dma((3,)),
         ],
         compiler_params=pltpu.CompilerParams(
             collective_id=1, has_side_effects=True, vmem_limit_bytes=48 << 20
         ),
         name="fold",
-    )(ret, onehot_t, terms)
+    )(ret, onehot_t, *terms)
 
 
 def per_device(
@@ -347,25 +402,19 @@
         jnp.einsum("rf,df->rd", grad_gate, w_gate[0], preferred_element_type=f32)
         + jnp.einsum("rf,df->rd", grad_up, w_up[0], preferred_element_type=f32)
     ).astype(bf16)
-    terms = jnp.stack(
-        [
-            jnp.einsum("rf,rd->fd", left, right, preferred_element_type=f32).astype(bf16)
-            for left, right in ((grad_gate, inputs), (grad_up, inputs), (hidden, cot))
-        ]
-    )
-
-    d_tokens, got = fold(
+    terms = [
+        jnp.einsum("rf,rd->fd", left, right, preferred_element_type=f32).astype(bf16)
+        for left, right in ((grad_gate, inputs), (grad_up, inputs), (hidden, cot))
+    ]
+
+    d_tokens, sum_gate, sum_up, sum_down = fold(
         ret.reshape(NEAR, RING, PAD, width), jnp.swapaxes(recv_g, 1, 2), terms
     )
-    mine = lax.dynamic_slice_in_dim(
-        terms, lax.axis_index("grp") * got.shape[3], got.shape[3], axis=2
-    )
-    sums = (jnp.sum(got.astype(f32), axis=0) + mine.astype(f32)).astype(bf16)
     return (
         d_tokens,
-        jnp.swapaxes(sums[0], 0, 1)[None],
-        jnp.swapaxes(sums[1], 0, 1)[None],
-        sums[2][None],
+        jnp.swapaxes(sum_gate, 0, 1)[None],
+        jnp.swapaxes(sum_up, 0, 1)[None],
+        sum_down[None],
     )
 
 

time: 436 us -> 332 us (0.76)
  Pallas kernels: 359 us -> 267 us
  other arithmetic: 21 us -> 9.65 us
    pallas_call x1, Pallas kernels: 181 us -> 89.3 us  [fold(): pl.pallas_call(fold_kernel, out_shape=(jax.ShapeDtypeStruct((rows, width)...]
    reduce_sum x1 -> x0, other arithmetic: 5.8 us -> none  [per_device(): sums = (jnp.sum(got.astype(f32), axis=0) + mine.astype(f32)).astype(bf16)]
    dot_general x3, matrix products: 10.6 us -> 16.2 us  [per_device(): jnp.einsum('rf,rd->fd', left, right, preferred_element_type=f32)]
    unnamed x37 -> x28, local copies, waits for them, and re-layouts: 9.23 us -> 9.82 us
where the time goes in v2:
time: 332 us; the launch traced here: 330 us
  Pallas kernels  267 us (80%)
  matrix products  33.7 us (10%)
  local copies, waits for them, and re-layouts  19.2 us (6%)
  other arithmetic  9.65 us (3%)
    pallas_call x1, Pallas kernels, spread(): pl.pallas_call(spread_kernel, out_shape=(landed, landed, jax.ShapeDtypeSt...  178 us
    pallas_call x1, Pallas kernels, fold(): pl.pallas_call(fold_kernel, out_shape=(jax.ShapeDtypeStruct((rows, width)...  89.3 us
    dot_general x3, matrix products, per_device(): jnp.einsum('rf,rd->fd', left, right, preferred_element_type=f32)  16.2 us
    unnamed x28, local copies, waits for them, and re-layouts  9.82 us

profile of v2, /device:TPU:1, one launch (start us, length us, event | category | flops | bytes accessed | tf_op | source)
XLA Modules:
  0.0 330.4 jit_solution(5700344974472194553)
XLA Ops:
  0.7 0.8 convert_element_type.69
  2.5 0.7 select_reduce_fusion.1
  3.6 0.7 iota_compare_fusion.1
  5.0 2.7 convolution_bitcast_fusion
  7.7 1.3 convolution_bitcast_fusion.1
  9.0 1.9 pad_maximum_fusion
  10.9 4.5 %copy.29 = bf16[1024,1408]{1,0:T(8,128)(2,1)} copy(bf16[1024,1408]{0,1:T(8,128)(2,1)} %pad_maximum_fusion) | data formatting | bytes 5767168 | tf_op jit(solution)/shard_map/concatenate | solution.py:381
  15.5 3.8 %pad_add_fusion.pre_ref = bf16[32,32,1408]{2,1,0:T(8,128)(2,1)} fusion(bf16[32,32,1408]{2,1,0:T(8,128)(2,1)} %bitcast.64, bf16[32,1,32]{2,1,0:T(2,128)(2,1)S(1)} %copy.30), kind=kLoop, calls=%fused_computation.25 | loop fusion | flops 5767168 | bytes 5769216 | tf_op jit(solution)/shard_map/add | solution.py:383
  19.3 177.6 %spread.1 = (bf16[4,8,32,2048]{3,2,1,0:T(8,128)(2,1)}, bf16[4,8,32,2048]{3,2,1,0:T(8,128)(2,1)}, bf16[4,8,32,1408]{3,2,1,0:T(8,128)(2,1)S(1)}, bf16[8,128,128]{2,1,0:T(8,128)(2,1)S(1)}) custom-call(bf16[128,2048]{1,0:T(8,128)(2,1)S(1)} %copy-done.2, bf16[128,2048]{1,0:T(8,128)(2,1)S(1)} %copy-done.3, bf16[8,128,128]{2,1,0:T(8,128)(2,1)S(1)} %fusion.16.g_ref, ...), custom_call_target="tpu_custom_call" | custom-call | tf_op jit(solution)/shard_map/spread/pallas_call | solution.py:288
  196.8 1.6 copy-done.1
  198.8 4.4 %fusion.26 = (bf16[1024,704]{1,0:T(8,128)(2,1)}, bf16[1024,704]{1,0:T(8,128)(2,1)}) fusion(bf16[1024,1408]{1,0:T(8,128)(2,1)} %bitcast.59), kind=kLoop, calls=%fused_computation.51 | loop fusion | bytes 5767168 | tf_op jit(solution)/shard_map/slice | solution.py:393
  203.2 2.6 copy.35
  205.8 2.6 copy.34
  208.4 8.3 %convolution_convert_fusion.wd_ref = bf16[704,2048]{1,0:T(8,128)(2,1)} fusion(bf16[1024,2048]{1,0:T(8,128)(2,1)} %bitcast.72, bf16[1024,704]{0,1:T(8,128)(2,1)} %copy.34, f32[1024]{0:T(1024)S(1)} %reshape.68, bf16[1024,704]{0,1:T(8,128)(2,1)} %copy.35), kind=kOutput, calls=%fused_computation.6 | convolution fusion | flops 2960719872 | bytes 9965568 | tf_op jit(solution)/shard_map/rf,rd->fd/dot_general | solution.py:406
  216.7 4.2 %multiply_convert_fusion = (bf16[1024,704]{0,1:T(8,128)(2,1)S(1)}, bf16[1024,704]{0,1:T(8,128)(2,1)S(1)}) fusion(f32[1024]{0:T(1024)S(1)} %reshape.68, bf16[1024,704]{0,1:T(8,128)(2,1)S(1)} %copy-done.4, bf16[1024,704]{0,1:T(8,128)(2,1)S(1)} %copy-done.5, bf16[1024,2048]{1,0:T(8,128)(2,1)S(1)} %bitcast.73, bf16[1,704,2048]{2,1,0:T(8,128)(2,1)S(1)} %copy-done.8), kind=kOutput, calls=%fused_computation.24 | convolution fusion | flops 2964324352 | bytes 12849152 | tf_op jit(solution)/shard_map/rd,fd->rf/dot_general | solution.py:398
  220.9 4.5 %convolution_convert_fusion.1.wu_ref = bf16[704,2048]{1,0:T(8,128)(2,1)} fusion(bf16[1024,704]{0,1:T(8,128)(2,1)S(1)} %get-tuple-element.20, bf16[1024,2048]{1,0:T(8,128)(2,1)S(1)} %bitcast.70), kind=kOutput, calls=%fused_computation.7 | convolution fusion | flops 2954231808 | bytes 8519680 | tf_op jit(solution)/shard_map/rf,rd->fd/dot_general | solution.py:406
  225.5 3.3 %convolution_convert_fusion.2.wg_ref = bf16[704,2048]{1,0:T(8,128)(2,1)S(1)} fusion(bf16[1024,704]{0,1:T(8,128)(2,1)S(1)} %get-tuple-element.21, bf16[1024,2048]{1,0:T(8,128)(2,1)S(1)} %bitcast.71), kind=kOutput, calls=%fused_computation.8 | convolution fusion | flops 2954231808 | bytes 8519680 | tf_op jit(solution)/shard_map/rf,rd->fd/dot_general | solution.py:406
  228.9 3.5 %fusion.9 = f32[1024,2048]{1,0:T(8,128)S(1)} fusion(bf16[1024,704]{0,1:T(8,128)(2,1)S(1)} %get-tuple-element.21, bf16[1,2048,704]{1,2,0:T(8,128)(2,1)S(1)} %copy-done), kind=kOutput, calls=%fused_computation.20 | convolution fusion | flops 2952790016 | bytes 12713984 | tf_op jit(solution)/shard_map/rf,df->rd/dot_general | solution.py:402
  232.4 5.6 %add_convert_fusion = bf16[1024,2048]{1,0:T(8,128)(2,1)} fusion(f32[1024,2048]{1,0:T(8,128)S(1)} %fusion.9, bf16[1024,704]{0,1:T(8,128)(2,1)S(1)} %get-tuple-element.20, bf16[1,2048,704]{1,2,0:T(8,128)(2,1)S(1)} %copy-done.9), kind=kOutput, calls=%fused_computation | convolution fusion | flops 2956984320 | bytes 16908288 | tf_op jit(solution)/shard_map/rf,df->rd/dot_general | solution.py:403
  238.0 89.3 %fold.1 = (bf16[128,2048]{1,0:T(8,128)(2,1)S(1)}, bf16[704,256]{1,0:T(8,128)(2,1)S(1)}, bf16[704,256]{1,0:T(8,128)(2,1)S(1)}, bf16[704,256]{1,0:T(8,128)(2,1)S(1)}) custom-call(bf16[4,8,32,2048]{3,2,1,0:T(8,128)(2,1)} %bitcast.65, bf16[8,128,128]{2,1,0:T(8,128)(2,1)S(1)} %bitcast.60, bf16[704,2048]{1,0:T(8,128)(2,1)S(1)} %convolution_convert_fusion.2.wg_ref, ...), custom_call_target="tpu_custom_call" | custom-call | tf_op jit(solution)/shard_map/fold/pallas_call | solution.py:328
  327.3 0.8 copy.45
  328.1 0.7 copy.46
  328.9 0.7 copy.47
  329.6 0.7 copy.48
  (36 shorter events, 2.4 us)
Async XLA Ops:
  0.6 228.2 %copy-start = (bf16[1,2048,704]{1,2,0:T(8,128)(2,1)S(1)}, bf16[1,2048,704]{1,2,0:T(8,128)(2,1)}, u32[]{:S(2)}) copy-start(bf16[1,2048,704]{1,2,0:T(8,128)(2,1)} %param.15) | copy-start | bytes 8650756
  5.0 2.7 copy-start.10
  15.5 3.8 %copy-start.2 = (bf16[128,2048]{1,0:T(8,128)(2,1)S(1)}, bf16[128,2048]{1,0:T(8,128)(2,1)}, u32[]{:S(2)}) copy-start(bf16[128,2048]{1,0:T(8,128)(2,1)} %d_ref.1) | copy-start | bytes 1572868
  15.5 3.8 %copy-start.3 = (bf16[128,2048]{1,0:T(8,128)(2,1)S(1)}, bf16[128,2048]{1,0:T(8,128)(2,1)}, u32[]{:S(2)}) copy-start(bf16[128,2048]{1,0:T(8,128)(2,1)} %t_ref.1) | copy-start | bytes 1572868
  196.8 1.6 copy-start.1
  208.4 8.3 %copy-start.4 = (bf16[1024,704]{0,1:T(8,128)(2,1)S(1)}, bf16[1024,704]{0,1:T(8,128)(2,1)}, u32[]{:S(2)}) copy-start(bf16[1024,704]{0,1:T(8,128)(2,1)} %copy.35) | copy-start | bytes 4325380
  208.4 8.3 %copy-start.5 = (bf16[1024,704]{0,1:T(8,128)(2,1)S(1)}, bf16[1024,704]{0,1:T(8,128)(2,1)}, u32[]{:S(2)}) copy-start(bf16[1024,704]{0,1:T(8,128)(2,1)} %copy.34) | copy-start | bytes 4325380
  208.4 8.3 %copy-start.7 = (bf16[4,8,32,2048]{3,2,1,0:T(8,128)(2,1)S(1)}, bf16[4,8,32,2048]{3,2,1,0:T(8,128)(2,1)}, u32[]{:S(2)}) copy-start(bf16[4,8,32,2048]{3,2,1,0:T(8,128)(2,1)} %get-tuple-element.13) | copy-start | bytes 12582916
  208.4 8.3 %copy-start.8 = (bf16[1,704,2048]{2,1,0:T(8,128)(2,1)S(1)}, bf16[1,704,2048]{2,1,0:T(8,128)(2,1)}, u32[]{:S(2)}) copy-start(bf16[1,704,2048]{2,1,0:T(8,128)(2,1)} %param.17) | copy-start | bytes 8650756
  216.7 4.2 %copy-start.6 = (bf16[4,8,32,2048]{3,2,1,0:T(8,128)(2,1)S(1)}, bf16[4,8,32,2048]{3,2,1,0:T(8,128)(2,1)}, u32[]{:S(2)}) copy-start(bf16[4,8,32,2048]{3,2,1,0:T(8,128)(2,1)} %get-tuple-element.15) | copy-start | bytes 12582916
  228.8 3.5 %copy-start.9 = (bf16[1,2048,704]{1,2,0:T(8,128)(2,1)S(1)}, bf16[1,2048,704]{1,2,0:T(8,128)(2,1)}, u32[]{:S(2)}) copy-start(bf16[1,2048,704]{1,2,0:T(8,128)(2,1)} %param.16) | copy-start | bytes 8650756

commit v3 on v2

--- a/solution.py
+++ b/solution.py
@@ -10,6 +10,8 @@
 NEAR = 4
 HOPS = RING // 2
 PAD = 32
+LOW = 64
+PRE_STAGES = ((3, 5), (4,), (2, 6), (1, 7, 0))
 SIDE = 4
 
 
@@ -44,8 +46,8 @@
 
 
 def spread_kernel(
-    d_ref, t_ref, g_ref, pre_ref, rd_ref, rt_ref, rpre_ref, rg_ref,
-    ring_d, ring_t, pick_d, pick_t, ring_s, ring_r, near_s, near_r, near_l, g_s, g_r, pre_s, pre_r, own_sem,
+    d_ref, t_ref, g_ref, route_ref, gate_ref, up_ref, rd_ref, rt_ref, rpre_ref, rg_ref,
+    table, pre, table_sem, ring_d, ring_t, pick_d, pick_t, ring_s, ring_r, near_s, near_r, near_l, g_s, g_r, pre_s, pre_r, own_sem,
 ):
     near, z = place()
     me = lax.axis_index("blk")
@@ -63,7 +65,10 @@
 
     own_refs, rings = (d_ref, t_ref), (ring_d, ring_t)
     picks, lands = (pick_d, pick_t), (rd_ref, rt_ref)
-    half = d_ref.shape[0] // 2
+    far = pl.ds(0, LOW), pl.ds(LOW, d_ref.shape[0] - LOW)
+
+    def ways(k):
+        return [way for way in range(2) if k < HOPS - 1 or far[way].size]
 
     def hop(a, way, k):
         step = 1 if way == 0 else -1
@@ -71,8 +76,8 @@
         src = own_refs[a] if k == 0 else rings[a].at[source]
         dst = rings[a].at[source]
         if k == HOPS - 1:
-            src = src.at[pl.ds(way * half, half)]
-            dst = dst.at[pl.ds(way * half, half)]
+            src = src.at[far[way]]
+            dst = dst.at[far[way]]
         return remote(
             src, dst, ring_s.at[a, way, k], ring_r.at[a, way, k], {"blk": at(near, wrap(z + step))}
         )
@@ -81,25 +86,53 @@
         to = wrap(z + k)
         return remote(g_ref.at[to], rg_ref.at[z], g_s.at[k], g_r.at[k], {"blk": at(near, to)})
 
-    def pre_copy(k):
-        to = lax.rem(me + k, count)
-        return remote(pre_ref.at[to], rpre_ref.at[near, z], pre_s.at[k], pre_r.at[k], {"blk": to})
+    def pre_copy(k, j):
+        to = at(lax.rem(near + j, NEAR), wrap(z + k))
+        return remote(pre.at[to], rpre_ref.at[near, z], pre_s.at[k, j], pre_r.at[k, j], {"blk": to})
+
+    def pre_each(number, act):
+        for k in PRE_STAGES[number]:
+            def one(j, carry, k=k):
+                act(pre_copy(k, j))
+                return carry
+
+            lax.fori_loop(0 if k else 1, NEAR, one, 0)
+
+    choices, ffw, rows = gate_ref.shape
+
+    def table_copy(i, k):
+        ref = (gate_ref, up_ref)[i]
+        dst = table.at[pl.ds(i * ffw, ffw), pl.ds(k * rows, rows)]
+        return pltpu.make_async_copy(ref.at[k], dst, table_sem.at[i, k])
 
     for a in range(2):
         for way in range(2):
             hop(a, way, 0).start()
+    for i in range(2):
+        for k in range(choices):
+            table_copy(i, k).start()
     for k in range(1, RING):
         g_copy(k).start()
     own_g = pltpu.make_async_copy(g_ref.at[z], rg_ref.at[z], own_sem.at[0])
     own_g.start()
-    own_pre = pltpu.make_async_copy(pre_ref.at[me], rpre_ref.at[near, z], own_sem.at[1])
+    for i in range(2):
+        for k in range(choices):
+            table_copy(i, k).wait()
+
+    def build(i, carry):
+        slots = pl.ds(pl.multiple_of(i * 8 * PAD, 8 * PAD), 8 * PAD)
+        take = jnp.concatenate([route_ref[k, slots, :] for k in range(choices)], axis=1)
+        taken = lax.dot_general(
+            take, table[...], (((1,), (1,)), ((), ())), preferred_element_type=jnp.float32
+        )
+        pre[pl.ds(i * 8, 8)] = taken.astype(jnp.bfloat16).reshape(8, PAD, 2 * ffw)
+        return carry
+
+    lax.fori_loop(0, count // 8, build, 0)
+    own_pre = pltpu.make_async_copy(pre.at[me], rpre_ref.at[near, z], own_sem.at[1])
     own_pre.start()
 
-    def pre_start(k, carry):
-        pre_copy(k).start()
-        return carry
-
-    lax.fori_loop(1, count, pre_start, 0)
+    pre_each(0, lambda copy: copy.start())
 
     def near_copy(a, source, number, j):
         to = lax.rem(near + j, NEAR)
@@ -113,7 +146,10 @@
 
     def gather(a, source, number):
         rows = own_refs[a][...] if number == 0 else rings[a][source]
-        taken = jnp.dot(rg_ref[source], rows, preferred_element_type=jnp.float32)
+        take = rg_ref[source]
+        if a == 1:
+            take = jnp.where(take.astype(jnp.float32) != 0.0, 1.0, 0.0).astype(jnp.bfloat16)
+        taken = jnp.dot(take, rows, preferred_element_type=jnp.float32)
         picks[a][source] = taken.astype(jnp.bfloat16).reshape(NEAR, PAD, taken.shape[1])
         for j in (1, 2, 3, 0):
             near_copy(a, source, number, j).start()
@@ -125,10 +161,12 @@
         g_copy(k).wait()
     for k in range(HOPS):
         for a in range(2):
-            for way in range(2):
+            for way in ways(k):
                 hop(a, way, k).wait_recv()
-                if k + 1 < HOPS:
+                if way in ways(k + 1) and k + 1 < HOPS:
                     hop(a, way, k + 1).start()
+            if a == 1 and k + 1 < HOPS:
+                pre_each(k + 1, lambda copy: copy.start())
             if k + 1 < HOPS:
                 gather(a, wrap(z - k - 1), 2 * k + 1)
                 gather(a, wrap(z + k + 1), 2 * k + 2)
@@ -137,14 +175,11 @@
 
     own_pre.wait()
 
-    def pre_wait(k, carry):
-        pre_copy(k).wait()
-        return carry
-
-    lax.fori_loop(1, count, pre_wait, 0)
+    for number in range(HOPS):
+        pre_each(number, lambda copy: copy.wait())
     for a in range(2):
-        for way in range(2):
-            for k in range(HOPS):
+        for k in range(HOPS):
+            for way in ways(k):
                 hop(a, way, k).wait_send()
         for number in range(RING):
             offset = (number + 1) // 2
@@ -280,22 +315,26 @@
         x_copy(t).wait_send()
 
 
-def spread(d_out, tokens, onehot, pre):
+def spread(d_out, tokens, onehot, route, gate_pre, up_pre):
     rows, width = d_out.shape
     bf16, dma = jnp.bfloat16, pltpu.SemaphoreType.DMA
     vmem, anywhere = pl.BlockSpec(memory_space=pltpu.VMEM), pl.BlockSpec(memory_space=pl.ANY)
     landed = jax.ShapeDtypeStruct((NEAR, RING, PAD, width), bf16)
+    choices, ffw = gate_pre.shape[:2]
     return pl.pallas_call(
         spread_kernel,
         out_shape=(
             landed,
             landed,
-            jax.ShapeDtypeStruct((NEAR, RING) + pre.shape[1:], bf16),
+            jax.ShapeDtypeStruct((NEAR, RING, PAD, 2 * ffw), bf16),
             jax.ShapeDtypeStruct(onehot.shape, bf16),
         ),
-        in_specs=[vmem, vmem, vmem, anywhere],
+        in_specs=[vmem, vmem, vmem, vmem, anywhere, anywhere],
         out_specs=(vmem, vmem, anywhere, vmem),
         scratch_shapes=[
+            pltpu.VMEM((2 * ffw, choices * rows), bf16),
+            pltpu.VMEM((NEAR * RING, PAD, 2 * ffw), bf16),
+            dma((2, choices)),
             pltpu.VMEM((RING, rows, width), bf16),
             pltpu.VMEM((RING, rows, width), bf16),
             pltpu.VMEM((RING, NEAR, PAD, width), bf16),
@@ -307,15 +346,15 @@
             dma((2, RING)),
             dma((RING,)),
             dma((RING,)),
-            dma((NEAR * RING,)),
-            dma((NEAR * RING,)),
+            dma((RING, NEAR)),
+            dma((RING, NEAR)),
             dma((2,)),
         ],
         compiler_params=pltpu.CompilerParams(
             collective_id=0, has_side_effects=True, vmem_limit_bytes=48 << 20
         ),
         name="spread",
-    )(d_out, tokens, onehot, pre)
+    )(d_out, tokens, onehot, route, gate_pre, up_pre)
 
 
 def fold(ret, onehot_t, terms):
@@ -368,34 +407,25 @@
     rank = jnp.dot(before, hit.astype(bf16), preferred_element_type=f32).astype(jnp.int32)
     slot = jnp.where(hit, rank, PAD).T
     onehot = (slot[:, None, :] == jnp.arange(PAD, dtype=jnp.int32)[None, :, None])
-    by_z = onehot.astype(bf16).reshape(2, RING, 2, PAD, rows)
+    gate_of = jnp.sum(jnp.where(chosen, gate_values.astype(f32)[:, :, None], 0.0), axis=1).T
+    by_z = jnp.where(onehot, gate_of[:, None, :], 0.0).astype(bf16).reshape(2, RING, 2, PAD, rows)
     by_z = jnp.transpose(by_z, (1, 0, 2, 3, 4)).reshape(RING, NEAR * PAD, rows)
     route = (onehot[None] & chosen.transpose(1, 2, 0)[:, :, None, :]).astype(bf16)
     route = route.reshape(-1, experts * PAD, rows)
-    picked = [
-        jnp.einsum("kst,tkf->sf", route, table, preferred_element_type=bf16)
-        for table in (saved_gate_pre, saved_up_pre)
-    ]
-    gate_of = jnp.sum(jnp.where(chosen, gate_values.astype(f32)[:, :, None], 0.0), axis=1).T
-    gate_slot = jnp.sum(jnp.where(onehot, gate_of[:, None, :], 0.0), axis=2)
-    pre = jnp.concatenate(picked, axis=1).reshape(experts, PAD, 2 * ffw)
-    slots = 13 * rows // (2 * experts)
-    pre = pre + jnp.pad(
-        gate_slot.astype(bf16)[:, None, :], ((0, 0), (slots, PAD - slots - 1), (0, 2 * ffw - PAD))
-    )
-
-    recv_d, recv_t, recv_pre, recv_g = spread(d_out, tokens, by_z, pre)
+
+    recv_d, recv_t, recv_pre, recv_g = spread(
+        d_out, tokens, by_z, route, *(jnp.transpose(a, (1, 2, 0)) for a in (saved_gate_pre, saved_up_pre))
+    )
 
     cot = recv_d.reshape(experts * PAD, width)
     inputs = recv_t.reshape(experts * PAD, width)
-    weights = recv_pre[:, :, slots, :PAD].astype(f32).reshape(experts * PAD, 1)
     recv_pre = recv_pre.reshape(experts * PAD, 2 * ffw)
     gate_pre = recv_pre[:, :ffw].astype(f32)
     up_pre = recv_pre[:, ffw:].astype(f32)
     sig = jax.nn.sigmoid(gate_pre)
     active = gate_pre * sig
-    hidden = (weights * active * up_pre).astype(bf16)
-    back = weights * jnp.einsum("rd,fd->rf", cot, w_down[0], preferred_element_type=f32)
+    hidden = (active * up_pre).astype(bf16)
+    back = jnp.einsum("rd,fd->rf", cot, w_down[0], preferred_element_type=f32)
     grad_gate = (back * up_pre * sig * (1.0 + gate_pre * (1.0 - sig))).astype(bf16)
     grad_up = (back * active).astype(bf16)
     ret = (
@@ -408,7 +438,7 @@
     ]
 
     d_tokens, sum_gate, sum_up, sum_down = fold(
-        ret.reshape(NEAR, RING, PAD, width), jnp.swapaxes(recv_g, 1, 2), terms
+        ret.reshape(NEAR, RING, PAD, width), jnp.swapaxes(recv_g != 0, 1, 2).astype(bf16), terms
     )
     return (
         d_tokens,

time: 332 us -> 313 us (0.943)
  other arithmetic: 9.65 us -> 3.87 us
  Pallas kernels: 267 us -> 262 us
  local copies, waits for them, and re-layouts: 19.2 us -> 15 us
    pallas_call x1, Pallas kernels: 178 us -> 172 us  [spread(): pl.pallas_call(spread_kernel, out_shape=(landed, landed, jax.ShapeDtypeSt...]
    concatenate x1 -> x0, local copies, waits for them, and re-layouts: 4.54 us -> none  [per_device(): pre = jnp.concatenate(picked, axis=1).reshape(experts, PAD, 2 * ffw)]
    dot_general x3 -> x1, matrix products: 8.19 us -> 3.89 us  [per_device(): back = jnp.einsum('rd,fd->rf', cot, w_down[0], preferred_element_type=f32)]
    add x1 -> x0, other arithmetic: 3.78 us -> none  [per_device(): pre + jnp.pad(gate_slot.astype(bf16)[:, None, :], ((0, 0), (slots, PAD -...]
    unnamed x28 -> x30, local copies, waits for them, and re-layouts: 9.82 us -> 10.3 us
where the time goes in v3:
time: 313 us
  Pallas kernels  262 us (84%)
  matrix products  31 us (10%)
  local copies, waits for them, and re-layouts  15 us (5%)
  other arithmetic  3.87 us (1%)
    pallas_call x1, Pallas kernels, spread(): pl.pallas_call(spread_kernel, out_shape=(landed, landed, jax.ShapeDtypeSt...  172 us
    pallas_call x1, Pallas kernels, fold(): pl.pallas_call(fold_kernel, out_shape=(jax.ShapeDtypeStruct((rows, width)...  90.5 us
    dot_general x3, matrix products, per_device(): jnp.einsum('rf,rd->fd', left, right, preferred_element_type=f32)  16.2 us
    unnamed x30, local copies, waits for them, and re-layouts  10.3 us
    dot_general x1, matrix products, per_device(): jnp.einsum('rf,df->rd', grad_up, w_up[0], preferred_element_type=f32)  7.26 us

profile of v3, /device:TPU:1, one launch (start us, length us, event | category | flops | bytes accessed | tf_op | source)
XLA Modules:
  0.0 312.8 jit_solution(17638885279140819787)
XLA Ops:
  0.7 0.8 convert_element_type.51
  1.6 0.7 select_reduce_fusion
  2.3 0.7 fusion.18
  3.0 0.2 fusion.15
  3.3 0.9 iota_compare_fusion
  4.2 0.2 bitcast_compare_fusion
  4.5 0.4 fusion.route_ref
  4.9 1.0 copy-done.3
  5.9 1.0 copy-done.4
  7.0 171.6 %spread.1 = (bf16[4,8,32,2048]{3,2,1,0:T(8,128)(2,1)}, bf16[4,8,32,2048]{3,2,1,0:T(8,128)(2,1)}, bf16[4,8,32,1408]{3,2,1,0:T(8,128)(2,1)}, bf16[8,128,128]{2,1,0:T(8,128)(2,1)S(1)}) custom-call(bf16[128,2048]{1,0:T(8,128)(2,1)S(1)} %copy-done.3, bf16[128,2048]{1,0:T(8,128)(2,1)S(1)} %copy-done.4, bf16[8,128,128]{2,1,0:T(8,128)(2,1)S(1)} %fusion.16.g_ref, ...), custom_call_target="tpu_custom_call" | custom-call | tf_op jit(solution)/shard_map/spread/pallas_call | solution.py:324
  178.8 4.4 %fusion.27 = (bf16[1024,704]{1,0:T(8,128)(2,1)}, bf16[1024,704]{1,0:T(8,128)(2,1)}) fusion(bf16[1024,1408]{1,0:T(8,128)(2,1)} %bitcast.64), kind=kLoop, calls=%fused_computation.46 | loop fusion | bytes 5767168 | tf_op jit(solution)/shard_map/slice | solution.py:423
  183.2 2.6 copy.32
  185.8 2.6 copy.31
  188.4 8.2 %convolution_convert_fusion.wd_ref = bf16[704,2048]{1,0:T(8,128)(2,1)} fusion(bf16[1024,2048]{1,0:T(8,128)(2,1)} %bitcast.70, bf16[1024,704]{0,1:T(8,128)(2,1)} %copy.31, bf16[1024,704]{0,1:T(8,128)(2,1)} %copy.32), kind=kOutput, calls=%fused_computation.6 | convolution fusion | flops 2959998976 | bytes 9961472 | tf_op jit(solution)/shard_map/rf,rd->fd/dot_general | solution.py:436
  196.7 3.9 %fusion.3 = (bf16[1024,704]{0,1:T(8,128)(2,1)S(1)}, f32[1024,704]{0,1:T(8,128)S(1)}) fusion(bf16[1024,704]{0,1:T(8,128)(2,1)S(1)} %copy-done.6, bf16[1024,704]{0,1:T(8,128)(2,1)S(1)} %copy-done.5, bf16[1024,2048]{1,0:T(8,128)(2,1)S(1)} %bitcast.71, bf16[1,704,2048]{2,1,0:T(8,128)(2,1)S(1)} %copy-done.9), kind=kOutput, calls=%fused_computation.13 | convolution fusion | flops 2961440768 | bytes 14286848 | tf_op jit(solution)/shard_map/rd,fd->rf/dot_general | solution.py:428
  200.6 3.4 %convolution_convert_fusion.2.wg_ref = bf16[704,2048]{1,0:T(8,128)(2,1)S(1)} fusion(bf16[1024,704]{0,1:T(8,128)(2,1)S(1)} %get-tuple-element.22, bf16[1024,2048]{1,0:T(8,128)(2,1)S(1)} %bitcast.68), kind=kOutput, calls=%fused_computation.8 | convolution fusion | flops 2954231808 | bytes 8519680 | tf_op jit(solution)/shard_map/rf,rd->fd/dot_general | solution.py:436
  203.9 4.6 %convolution_convert_fusion.1.wu_ref = bf16[704,2048]{1,0:T(8,128)(2,1)} fusion(bf16[1024,2048]{1,0:T(8,128)(2,1)S(1)} %bitcast.69, f32[1024,704]{0,1:T(8,128)S(1)} %get-tuple-element.23, bf16[1024,704]{0,1:T(8,128)(2,1)S(1)} %copy-done.5), kind=kOutput, calls=%fused_computation.7 | convolution fusion | flops 2959278080 | bytes 11403264 | tf_op jit(solution)/shard_map/rf,rd->fd/dot_general | solution.py:436
  208.6 3.5 %fusion.10 = f32[1024,2048]{1,0:T(8,128)S(1)} fusion(bf16[1024,704]{0,1:T(8,128)(2,1)S(1)} %get-tuple-element.22, bf16[1,2048,704]{1,2,0:T(8,128)(2,1)S(1)} %copy-done), kind=kOutput, calls=%fused_computation.20 | convolution fusion | flops 2952790016 | bytes 12713984 | tf_op jit(solution)/shard_map/rf,df->rd/dot_general | solution.py:432
  212.1 7.3 %add_convert_fusion = bf16[1024,2048]{1,0:T(8,128)(2,1)} fusion(f32[1024,2048]{1,0:T(8,128)S(1)} %fusion.10, bf16[1,2048,704]{1,2,0:T(8,128)(2,1)S(1)} %copy-done.10, f32[1024,704]{0,1:T(8,128)} %copy-done.11, bf16[1024,704]{0,1:T(8,128)(2,1)S(1)} %copy-done.5), kind=kOutput, calls=%fused_computation | convolution fusion | flops 2962030592 | bytes 19791872 | tf_op jit(solution)/shard_map/rf,df->rd/dot_general | solution.py:433
  219.3 90.5 %fold.1 = (bf16[128,2048]{1,0:T(8,128)(2,1)S(1)}, bf16[704,256]{1,0:T(8,128)(2,1)S(1)}, bf16[704,256]{1,0:T(8,128)(2,1)S(1)}, bf16[704,256]{1,0:T(8,128)(2,1)S(1)}) custom-call(bf16[4,8,32,2048]{3,2,1,0:T(8,128)(2,1)} %bitcast.63, bf16[8,128,128]{2,1,0:T(8,128)(2,1)S(1)} %fusion.17.g_ref, bf16[704,2048]{1,0:T(8,128)(2,1)S(1)} %convolution_convert_fusion.2.wg_ref, ...), custom_call_target="tpu_custom_call" | custom-call | tf_op jit(solution)/shard_map/fold/pallas_call | solution.py:367
  309.8 0.8 copy.41
  310.6 0.7 copy.42
  311.4 0.7 copy.43
  312.1 0.7 copy.44
  (30 shorter events, 0.6 us)
Async XLA Ops:
  0.6 207.9 %copy-start = (bf16[1,2048,704]{1,2,0:T(8,128)(2,1)S(1)}, bf16[1,2048,704]{1,2,0:T(8,128)(2,1)}, u32[]{:S(2)}) copy-start(bf16[1,2048,704]{1,2,0:T(8,128)(2,1)} %param.15) | copy-start | bytes 8650756
  3.3 1.6 copy-start.1
  3.3 1.6 copy-start.2
  4.9 1.0 copy-start.3
  5.9 1.0 copy-start.4
  188.4 8.3 %copy-start.5 = (bf16[1024,704]{0,1:T(8,128)(2,1)S(1)}, bf16[1024,704]{0,1:T(8,128)(2,1)}, u32[]{:S(2)}) copy-start(bf16[1024,704]{0,1:T(8,128)(2,1)} %copy.32) | copy-start | bytes 4325380
  188.4 8.3 %copy-start.6 = (bf16[1024,704]{0,1:T(8,128)(2,1)S(1)}, bf16[1024,704]{0,1:T(8,128)(2,1)}, u32[]{:S(2)}) copy-start(bf16[1024,704]{0,1:T(8,128)(2,1)} %copy.31) | copy-start | bytes 4325380
  188.4 8.3 %copy-start.8 = (bf16[4,8,32,2048]{3,2,1,0:T(8,128)(2,1)S(1)}, bf16[4,8,32,2048]{3,2,1,0:T(8,128)(2,1)}, u32[]{:S(2)}) copy-start(bf16[4,8,32,2048]{3,2,1,0:T(8,128)(2,1)} %get-tuple-element.12) | copy-start | bytes 12582916
  188.4 8.3 %copy-start.9 = (bf16[1,704,2048]{2,1,0:T(8,128)(2,1)S(1)}, bf16[1,704,2048]{2,1,0:T(8,128)(2,1)}, u32[]{:S(2)}) copy-start(bf16[1,704,2048]{2,1,0:T(8,128)(2,1)} %param.17) | copy-start | bytes 8650756
  196.6 3.9 %copy-start.7 = (bf16[4,8,32,2048]{3,2,1,0:T(8,128)(2,1)S(1)}, bf16[4,8,32,2048]{3,2,1,0:T(8,128)(2,1)}, u32[]{:S(2)}) copy-start(bf16[4,8,32,2048]{3,2,1,0:T(8,128)(2,1)} %get-tuple-element.15) | copy-start | bytes 12582916
  200.6 3.4 %copy-start.11 = (f32[1024,704]{0,1:T(8,128)}, f32[1024,704]{0,1:T(8,128)S(1)}, u32[]{:S(2)}) copy-start(f32[1024,704]{0,1:T(8,128)S(1)} %get-tuple-element.23) | copy-start | bytes 8650756
  208.6 3.5 %copy-start.10 = (bf16[1,2048,704]{1,2,0:T(8,128)(2,1)S(1)}, bf16[1,2048,704]{1,2,0:T(8,128)(2,1)}, u32[]{:S(2)}) copy-start(bf16[1,2048,704]{1,2,0:T(8,128)(2,1)} %param.16) | copy-start | bytes 8650756

commit v4 on v3

--- a/solution.py
+++ b/solution.py
@@ -419,21 +419,21 @@
 
     cot = recv_d.reshape(experts * PAD, width)
     inputs = recv_t.reshape(experts * PAD, width)
-    recv_pre = recv_pre.reshape(experts * PAD, 2 * ffw)
-    gate_pre = recv_pre[:, :ffw].astype(f32)
-    up_pre = recv_pre[:, ffw:].astype(f32)
+    recv_pre = recv_pre.reshape(experts * PAD, 2 * ffw).T
+    gate_pre = recv_pre[:ffw].astype(f32)
+    up_pre = recv_pre[ffw:].astype(f32)
     sig = jax.nn.sigmoid(gate_pre)
     active = gate_pre * sig
     hidden = (active * up_pre).astype(bf16)
-    back = jnp.einsum("rd,fd->rf", cot, w_down[0], preferred_element_type=f32)
+    back = jnp.einsum("fd,rd->fr", w_down[0], cot, preferred_element_type=f32)
     grad_gate = (back * up_pre * sig * (1.0 + gate_pre * (1.0 - sig))).astype(bf16)
     grad_up = (back * active).astype(bf16)
     ret = (
-        jnp.einsum("rf,df->rd", grad_gate, w_gate[0], preferred_element_type=f32)
-        + jnp.einsum("rf,df->rd", grad_up, w_up[0], preferred_element_type=f32)
+        jnp.einsum("fr,df->rd", grad_gate, w_gate[0], preferred_element_type=f32)
+        + jnp.einsum("fr,df->rd", grad_up, w_up[0], preferred_element_type=f32)
     ).astype(bf16)
     terms = [
-        jnp.einsum("rf,rd->fd", left, right, preferred_element_type=f32).astype(bf16)
+        jnp.einsum("fr,rd->fd", left, right, preferred_element_type=f32).astype(bf16)
         for left, right in ((grad_gate, inputs), (grad_up, inputs), (hidden, cot))
     ]
 

time: 313 us -> 308 us (0.984)
  local copies, waits for them, and re-layouts: 15 us -> 10.1 us
    unnamed x30 -> x26, local copies, waits for them, and re-layouts: 10.3 us -> 5.12 us
    reshape x0 -> x1, local copies, waits for them, and re-layouts: none -> 4.61 us  [per_device(): recv_pre = recv_pre.reshape(experts * PAD, 2 * ffw).T]
    slice x1 -> x0, local copies, waits for them, and re-layouts: 4.4 us -> none  [per_device(): gate_pre = recv_pre[:, :ffw].astype(f32)]
where the time goes in v4:
time: 308 us
  Pallas kernels  262 us (85%)
  matrix products  31 us (10%)
  local copies, waits for them, and re-layouts  10.1 us (3%)
  other arithmetic  3.87 us (1%)
    pallas_call x1, Pallas kernels, spread(): pl.pallas_call(spread_kernel, out_shape=(landed, landed, jax.ShapeDtypeSt...  172 us
    pallas_call x1, Pallas kernels, fold(): pl.pallas_call(fold_kernel, out_shape=(jax.ShapeDtypeStruct((rows, width)...  90.5 us
    dot_general x3, matrix products, per_device(): jnp.einsum('fr,rd->fd', left, right, preferred_element_type=f32)  16.4 us
    dot_general x1, matrix products, per_device(): jnp.einsum('fr,df->rd', grad_up, w_up[0], preferred_element_type=f32)  7.04 us

profile of v4, /device:TPU:1, one launch (start us, length us, event | category | flops | bytes accessed | tf_op | source)
XLA Modules:
  0.0 307.9 jit_solution(15271018320026315933)
XLA Ops:
  0.7 0.8 convert_element_type.51
  1.6 0.7 select_reduce_fusion
  2.3 0.7 fusion.20
  3.0 0.2 fusion.17
  3.3 0.9 iota_compare_fusion
  4.2 0.2 bitcast_compare_fusion
  4.4 0.1 fusion.18.g_ref
  4.5 0.4 fusion.route_ref
  4.9 1.0 copy-done.3
  5.9 1.0 copy-done.4
  7.0 171.6 %spread.1 = (bf16[4,8,32,2048]{3,2,1,0:T(8,128)(2,1)}, bf16[4,8,32,2048]{3,2,1,0:T(8,128)(2,1)}, bf16[4,8,32,1408]{3,2,1,0:T(8,128)(2,1)}, bf16[8,128,128]{2,1,0:T(8,128)(2,1)S(1)}) custom-call(bf16[128,2048]{1,0:T(8,128)(2,1)S(1)} %copy-done.3, bf16[128,2048]{1,0:T(8,128)(2,1)S(1)} %copy-done.4, bf16[8,128,128]{2,1,0:T(8,128)(2,1)S(1)} %fusion.18.g_ref, ...), custom_call_target="tpu_custom_call" | custom-call | tf_op jit(solution)/shard_map/spread/pallas_call | solution.py:324
  178.6 4.6 %copy.26 = bf16[1024,1408]{0,1:T(8,128)(2,1)} copy(bf16[1024,1408]{1,0:T(8,128)(2,1)} %bitcast.76) | data formatting | bytes 5767168 | tf_op jit(solution)/shard_map/reshape | solution.py:422
  183.2 0.2 copy.27
  183.5 8.2 %convolution_convert_fusion.wd_ref = bf16[704,2048]{1,0:T(8,128)(2,1)} fusion(bf16[1024,2048]{1,0:T(8,128)(2,1)} %bitcast.82, bf16[1408,1024]{1,0:T(8,128)(2,1)} %bitcast.72), kind=kOutput, calls=%fused_computation.6 | convolution fusion | flops 2959998976 | bytes 9961472 | tf_op jit(solution)/shard_map/fr,rd->fd/dot_general | solution.py:436
  191.7 3.9 %fusion.3 = (bf16[704,1024]{1,0:T(8,128)(2,1)S(1)}, f32[1024,704]{0,1:T(8,128)S(1)}) fusion(bf16[1408,1024]{1,0:T(8,128)(2,1)S(1)} %bitcast.73, bf16[1024,2048]{1,0:T(8,128)(2,1)S(1)} %bitcast.83, bf16[1,704,2048]{2,1,0:T(8,128)(2,1)S(1)} %copy-done.8), kind=kOutput, calls=%fused_computation.13 | convolution fusion | flops 2961440768 | bytes 14286848 | tf_op jit(solution)/shard_map/fd,rd->fr/dot_general | solution.py:428
  195.6 3.5 %convolution_convert_fusion.2.wg_ref = bf16[704,2048]{1,0:T(8,128)(2,1)S(1)} fusion(bf16[704,1024]{1,0:T(8,128)(2,1)S(1)} %get-tuple-element.20, bf16[1024,2048]{1,0:T(8,128)(2,1)S(1)} %bitcast.80), kind=kOutput, calls=%fused_computation.8 | convolution fusion | flops 2954231808 | bytes 8519680 | tf_op jit(solution)/shard_map/fr,rd->fd/dot_general | solution.py:436
  199.2 4.6 %convolution_convert_fusion.1.wu_ref = bf16[704,2048]{1,0:T(8,128)(2,1)} fusion(bf16[1024,2048]{1,0:T(8,128)(2,1)S(1)} %bitcast.81, f32[1024,704]{0,1:T(8,128)S(1)} %get-tuple-element.21, bf16[1408,1024]{1,0:T(8,128)(2,1)S(1)} %bitcast.74), kind=kOutput, calls=%fused_computation.7 | convolution fusion | flops 2959278080 | bytes 11403264 | tf_op jit(solution)/shard_map/fr,rd->fd/dot_general | solution.py:436
  203.8 3.5 %fusion.10 = f32[1024,2048]{1,0:T(8,128)S(1)} fusion(bf16[704,1024]{1,0:T(8,128)(2,1)S(1)} %get-tuple-element.20, bf16[1,2048,704]{1,2,0:T(8,128)(2,1)S(1)} %copy-done), kind=kOutput, calls=%fused_computation.20 | convolution fusion | flops 2952790016 | bytes 12713984 | tf_op jit(solution)/shard_map/fr,df->rd/dot_general | solution.py:432
  207.3 7.0 %add_convert_fusion = bf16[1024,2048]{1,0:T(8,128)(2,1)} fusion(f32[1024,2048]{1,0:T(8,128)S(1)} %fusion.10, bf16[1,2048,704]{1,2,0:T(8,128)(2,1)S(1)} %copy-done.9, f32[1024,704]{0,1:T(8,128)} %copy-done.10, bf16[1408,1024]{1,0:T(8,128)(2,1)S(1)} %bitcast.75), kind=kOutput, calls=%fused_computation | convolution fusion | flops 2962030592 | bytes 19791872 | tf_op jit(solution)/shard_map/fr,df->rd/dot_general | solution.py:433
  214.4 90.5 %fold.1 = (bf16[128,2048]{1,0:T(8,128)(2,1)S(1)}, bf16[704,256]{1,0:T(8,128)(2,1)S(1)}, bf16[704,256]{1,0:T(8,128)(2,1)S(1)}, bf16[704,256]{1,0:T(8,128)(2,1)S(1)}) custom-call(bf16[4,8,32,2048]{3,2,1,0:T(8,128)(2,1)} %bitcast.71, bf16[8,128,128]{2,1,0:T(8,128)(2,1)S(1)} %fusion.19.g_ref, bf16[704,2048]{1,0:T(8,128)(2,1)S(1)} %convolution_convert_fusion.2.wg_ref, ...), custom_call_target="tpu_custom_call" | custom-call | tf_op jit(solution)/shard_map/fold/pallas_call | solution.py:367
  304.9 0.8 copy.36
  305.7 0.7 copy.37
  306.4 0.7 copy.38
  307.1 0.7 copy.39
  (26 shorter events, 0.3 us)
Async XLA Ops:
  0.6 203.2 %copy-start = (bf16[1,2048,704]{1,2,0:T(8,128)(2,1)S(1)}, bf16[1,2048,704]{1,2,0:T(8,128)(2,1)}, u32[]{:S(2)}) copy-start(bf16[1,2048,704]{1,2,0:T(8,128)(2,1)} %param.15) | copy-start | bytes 8650756
  3.3 1.6 copy-start.1
  3.3 1.6 copy-start.2
  4.9 1.0 copy-start.3
  5.9 1.0 copy-start.4
  183.4 8.3 %copy-start.5 = (bf16[1024,1408]{0,1:T(8,128)(2,1)S(1)}, bf16[1024,1408]{0,1:T(8,128)(2,1)}, u32[]{:S(2)}) copy-start(bf16[1024,1408]{0,1:T(8,128)(2,1)} %copy.26) | copy-start | bytes 8650756
  183.4 8.3 %copy-start.7 = (bf16[4,8,32,2048]{3,2,1,0:T(8,128)(2,1)S(1)}, bf16[4,8,32,2048]{3,2,1,0:T(8,128)(2,1)}, u32[]{:S(2)}) copy-start(bf16[4,8,32,2048]{3,2,1,0:T(8,128)(2,1)} %get-tuple-element.12) | copy-start | bytes 12582916
  183.4 8.2 %copy-start.8 = (bf16[1,704,2048]{2,1,0:T(8,128)(2,1)S(1)}, bf16[1,704,2048]{2,1,0:T(8,128)(2,1)}, u32[]{:S(2)}) copy-start(bf16[1,704,2048]{2,1,0:T(8,128)(2,1)} %param.17) | copy-start | bytes 8650756
  191.7 3.9 %copy-start.6 = (bf16[4,8,32,2048]{3,2,1,0:T(8,128)(2,1)S(1)}, bf16[4,8,32,2048]{3,2,1,0:T(8,128)(2,1)}, u32[]{:S(2)}) copy-start(bf16[4,8,32,2048]{3,2,1,0:T(8,128)(2,1)} %get-tuple-element.15) | copy-start | bytes 12582916
  195.6 3.6 %copy-start.10 = (f32[1024,704]{0,1:T(8,128)}, f32[1024,704]{0,1:T(8,128)S(1)}, u32[]{:S(2)}) copy-start(f32[1024,704]{0,1:T(8,128)S(1)} %get-tuple-element.21) | copy-start | bytes 8650756
  203.8 3.5 %copy-start.9 = (bf16[1,2048,704]{1,2,0:T(8,128)(2,1)S(1)}, bf16[1,2048,704]{1,2,0:T(8,128)(2,1)}, u32[]{:S(2)}) copy-start(bf16[1,2048,704]{1,2,0:T(8,128)(2,1)} %param.16) | copy-start | bytes 8650756
